TPU v7x, 32 devices: a whole 2x2x4 slice. The times are simulated.
32 devices in a mesh: user: 4 (over x, core), heads: 2 (over y), ctx: 4 (over z).
Axes of the slice: x: 2, y: 2, z: 4, core: 2. Of those that a mesh axis runs over, the one named last changes fastest.
Arguments:
- keys: bfloat16 [65536, 512], P(('user', 'ctx'), 'heads'), parts along dimension 0, may hold values from -6 to 6
- values: bfloat16 [65536, 512], P(('user', 'ctx'), 'heads'), parts along dimension 0, may hold values from -6 to 6
- queries: bfloat16 [4, 12288, 128], P('heads', ('user', 'ctx')), parts along dimension 1, may hold values from -240 to 240
- positions: int32 [12288], P(('user', 'ctx')), parts along dimension 0, may hold values from 0 to 16383
Outputs:
- attended: bfloat16 [4, 12288, 128], P('heads', ('user', 'ctx')), parts along dimension 1
There are 4 independent parts, one for each index of `user`. A program takes and returns all parts, laid end to end along the dimension named above; each array names one. Nothing has to cross between parts.
All inputs are finite; a program needn't handle non-finite values.
Results may differ from a plain program's by a relative error of at most 0.008.
The roundings to bfloat16 on the way count: a program that leaves them out, or rounds other values in their place, can miss the bound.
Values may be sent and summed in bfloat16 or wider, within the bound.
A program may use at most 128 MiB of HBM per device.

v0:
```python
import math

import jax
import jax.numpy as jnp
from jax import lax
from jax.sharding import PartitionSpec as P

FACTOR = 128


highest = lax.Precision.HIGHEST


def phases(first, second, period):
    product = (
        jnp.arange(first, dtype=jnp.int32)[:, None]
        * jnp.arange(second, dtype=jnp.int32)[None, :]
        % period
    )
    angles = 2.0 * math.pi / period * product.astype(jnp.float32)
    return (jnp.cos(angles), jnp.sin(angles))


def contract(form, left, right):
    return jnp.einsum(form, left, right, precision=highest)


def compress(signal):
    count_rows, length = signal.shape
    outer = FACTOR
    inner = length // outer
    reordered = jnp.concatenate([signal[:, 0::2], signal[:, 1::2][:, ::-1]], axis=1).reshape(
        count_rows, outer, inner
    )
    cos_outer, sin_outer = phases(outer, outer, outer)
    cos_twist, sin_twist = phases(outer, inner, length)
    cos_inner, sin_inner = phases(inner, inner // 2, inner)
    real_one = contract("rab,ac->rcb", reordered, cos_outer)
    imag_one = -contract("rab,ac->rcb", reordered, sin_outer)
    real_two = real_one * cos_twist + imag_one * sin_twist
    imag_two = imag_one * cos_twist - real_one * sin_twist
    real_three = contract("rcb,bd->rcd", real_two, cos_inner) + contract(
        "rcb,bd->rcd", imag_two, sin_inner
    )
    imag_three = contract("rcb,bd->rcd", imag_two, cos_inner) - contract(
        "rcb,bd->rcd", real_two, sin_inner
    )
    index = (jnp.arange(outer)[:, None] + outer * jnp.arange(inner // 2)[None, :]).astype(
        jnp.float32
    )
    coeffs = real_three * jnp.cos(math.pi * index / (2 * length)) + imag_three * jnp.sin(
        math.pi * index / (2 * length)
    )
    weight = jnp.where(index == 0.0, 1.0 / length, 2.0 / length)
    scaled = coeffs * weight
    real_four = scaled * jnp.cos(math.pi * index / length)
    imag_four = scaled * jnp.sin(math.pi * index / length)
    real_five = contract("rcd,bd->rcb", real_four, cos_inner) - contract(
        "rcd,bd->rcb", imag_four, sin_inner
    )
    imag_five = contract("rcd,bd->rcb", real_four, sin_inner) + contract(
        "rcd,bd->rcb", imag_four, cos_inner
    )
    real_six = real_five * cos_twist - imag_five * sin_twist
    imag_six = real_five * sin_twist + imag_five * cos_twist
    result = contract("rcb,ca->rab", real_six, cos_outer[:, : outer // 2]) - contract(
        "rcb,ca->rab", imag_six, sin_outer[:, : outer // 2]
    )
    return result.reshape(count_rows, length // 2)


def inverse_freq(width):
    return jnp.exp(jnp.arange(width // 2).astype(jnp.float32) * (-2.0 * math.log(500000.0) / width))


def rotate_rows(block, places):
    width = block.shape[-1]
    half = width // 2
    angles = places[:, None] * inverse_freq(width)[None, :]
    cosine = jnp.cos(angles)
    sine = jnp.sin(angles)
    first = block[..., :half]
    second = block[..., half:]
    return jnp.concatenate(
        [first * cosine - second * sine, second * cosine + first * sine], axis=-1
    )


def rotate_columns(block, places):
    width = block.shape[1]
    half = width // 2
    angles = inverse_freq(width)[:, None] * places[None, :]
    cosine = jnp.cos(angles)
    sine = jnp.sin(angles)
    first = block[:, :half]
    second = block[:, half:]
    return jnp.concatenate([first * cosine - second * sine, second * cosine + first * sine], axis=1)


def on_device(keys, values, queries, positions):
    key_parts, value_parts = (
        lax.all_to_all(keys, "ctx", split_axis=1, concat_axis=0, tiled=True),
        lax.all_to_all(values, "ctx", split_axis=1, concat_axis=0, tiled=True),
    )
    per_device = key_parts.shape[1]
    stacked = jnp.concatenate([key_parts, value_parts], axis=1).astype(jnp.float32).T
    compact = compress(stacked).astype(jnp.bfloat16)
    heads_here, query_count, head_width = queries.shape
    scaling = 1.0 / math.sqrt(head_width)
    rotated_queries = rotate_rows(
        queries.astype(jnp.float32), positions.astype(jnp.float32)
    ).astype(jnp.bfloat16)
    whole = lax.all_gather(compact, "ctx", axis=0, tiled=True)
    groups = whole.shape[0] // (2 * per_device)
    tokens_here = whole.shape[1]
    shaped = whole.reshape(groups, 2, per_device, tokens_here)
    key_rows = shaped[:, 0].reshape(heads_here, head_width, tokens_here)
    value_rows = shaped[:, 1].reshape(heads_here, head_width, tokens_here)
    key_rows, value_rows = (key_rows, value_rows)
    places = jnp.arange(whole.shape[1]).astype(jnp.float32)
    key_ready = rotate_columns(key_rows.astype(jnp.float32), places).astype(jnp.bfloat16)
    best = jnp.full((heads_here, query_count), -jnp.inf, jnp.float32)
    total = jnp.zeros((heads_here, query_count), jnp.float32)
    accum = jnp.zeros((heads_here, query_count, head_width), jnp.float32)
    scores = (
        jnp.einsum("hqd,hdn->hqn", rotated_queries, key_ready, preferred_element_type=jnp.float32)
        * scaling
    )
    fresh = jnp.max(scores, axis=2)
    shrink = jnp.exp(best - fresh)
    expo = jnp.exp(scores - fresh[:, :, None])
    total = total * shrink + jnp.sum(expo, axis=2)
    summed = jnp.einsum(
        "hqn,hdn->hqd", expo.astype(jnp.bfloat16), value_rows, preferred_element_type=jnp.float32
    )
    accum = accum * shrink[:, :, None] + summed
    best, total, accum = (fresh, total, accum)
    return (accum / total[:, :, None]).astype(jnp.bfloat16)


def solution(mesh):
    return jax.shard_map(
        on_device,
        mesh=mesh,
        in_specs=(
            P(("user", "ctx"), "heads"),
            P(("user", "ctx"), "heads"),
            P("heads", ("user", "ctx"), None),
            P(("user", "ctx")),
        ),
        out_specs=P("heads", ("user", "ctx"), None),
        check_vma=False,
    )
```

profile of v0, /device:TPU:0, one launch (start us, length us, event | category | flops | bytes accessed | tf_op | source)
XLA Modules:
  0.0 939.0 jit_solution(2521701143495355077)
XLA Ops:
  6.5 4.1 copy.21
  10.6 6.3 all-to-all-start
  17.0 4.1 copy.23
  21.1 44.1 %all-to-all-done = bf16[4096,4,64]{0,2,1:T(8,128)(2,1)S(1)} async-done(((bf16[4096,4,64]{0,2,1:T(8,128)(2,1)}), bf16[4096,4,64]{0,2,1:T(8,128)(2,1)S(1)}, u32[]{:S(2)}, u32[]{:S(2)}) %all-to-all-start) | async-done | bytes 2097184 | tf_op jit(solution)/shard_map/all_to_all | solution.py:102
  65.2 4.5 all-to-all-start.1
  69.6 0.0 all-gather.2.cloned.1.call-start
  69.7 0.3 fusion.93
  69.9 0.1 copy.25
  70.0 0.3 fusion.92
  70.3 0.1 copy.26
  70.4 0.3 fusion.95
  70.7 0.3 fusion.94
  70.9 0.3 fusion.88
  71.3 1.5 copy.33
  72.8 44.7 %all-to-all-done.1 = bf16[4096,4,64]{0,2,1:T(8,128)(2,1)} async-done(((bf16[4096,4,64]{0,2,1:T(8,128)(2,1)}), bf16[4096,4,64]{0,2,1:T(8,128)(2,1)}, u32[]{:S(2)}, u32[]{:S(2)}) %all-to-all-start.1) | async-done | bytes 2097184 | tf_op jit(solution)/shard_map/all_to_all | solution.py:103
  117.5 1.8 copy.34
  119.3 5.7 convert_bitcast_fusion
  124.9 185.3 %slice.34 = f32[128,8192]{1,0:T(8,128)} slice(f32[128,16384]{1,0:T(8,128)} %convert_bitcast_fusion), slice={[0:128:1], [1:16384:2]} | slice | bytes 8388608 | tf_op jit(solution)/shard_map/slice | solution.py:32
  310.2 185.1 %slice.33 = f32[128,8192]{1,0:T(8,128)} slice(f32[128,16384]{1,0:T(8,128)} %convert_bitcast_fusion), slice={[0:128:1], [0:16384:2]} | slice | bytes 8388608 | tf_op jit(solution)/shard_map/slice | solution.py:32
  495.3 34.6 %rev.3 = f32[128,8192]{1,0:T(8,128)} reverse(f32[128,8192]{1,0:T(8,128)} %slice.34), dimensions={1} | reverse | bytes 8388608 | tf_op jit(solution)/shard_map/rev | solution.py:32
  529.9 7.5 maximum_bitcast_fusion
  537.4 4.8 copy.35
  542.3 0.0 copy-start.1
  542.3 3.2 copy-done.1
  545.5 8.6 fusion.64
  554.1 11.1 %fusion.66 = f32[128,128,128]{2,0,1:T(8,128)S(1)} fusion(f32[128,128,128]{2,1,0:T(8,128)} %bitcast.72), kind=kOutput, calls=%fused_computation.77 | convolution fusion | flops 3221454848 | bytes 16777216 | tf_op jit(solution)/shard_map/rab,ac->rcb/dot_general | solution.py:25
  565.1 12.0 %fusion.4 = f32[128,128,64]{1,2,0:T(8,128)} fusion(f32[128,128,128]{2,0,1:T(8,128)S(1)} %fusion.66, f32[128,128,128]{2,0,1:T(8,128)S(1)} %fusion.64, f32[128,128]{1,0:T(8,128)S(1)} %copy.26, f32[128,128]{1,0:T(8,128)S(1)} %copy.25), kind=kOutput, calls=%fused_computation.6 | convolution fusion | flops 1619116032 | bytes 21102592 | tf_op jit(solution)/shard_map/rcb,bd->rcd/dot_general | solution.py:25
  577.1 12.1 %fusion.8 = f32[128,128,64]{1,2,0:T(8,128)} fusion(f32[128,128,128]{2,0,1:T(8,128)S(1)} %fusion.66, f32[128,128,128]{2,0,1:T(8,128)S(1)} %fusion.64, f32[128,128]{1,0:T(8,128)S(1)} %copy.26, f32[128,128]{1,0:T(8,128)S(1)} %copy.25), kind=kOutput, calls=%fused_computation.10 | convolution fusion | flops 1619116032 | bytes 21102592 | tf_op jit(solution)/shard_map/rcb,bd->rcd/dot_general | solution.py:25
  589.2 12.1 %fusion.6 = f32[128,128,64]{1,2,0:T(8,128)} fusion(f32[128,128,128]{2,0,1:T(8,128)S(1)} %fusion.66, f32[128,128,128]{2,0,1:T(8,128)S(1)} %fusion.64, f32[128,128]{1,0:T(8,128)S(1)} %copy.26, f32[128,128]{1,0:T(8,128)S(1)} %copy.25), kind=kOutput, calls=%fused_computation.8 | convolution fusion | flops 1619116032 | bytes 21102592 | tf_op jit(solution)/shard_map/rcb,bd->rcd/dot_general | solution.py:25
  601.3 14.8 %add_multiply_fusion = f32[128,128,64]{1,2,0:T(8,128)} fusion(f32[128,128,64]{1,2,0:T(8,128)} %fusion.4, f32[128,128,64]{1,2,0:T(8,128)} %fusion.8, f32[128,128,64]{1,2,0:T(8,128)} %fusion.6, f32[128,128,128]{2,0,1:T(8,128)S(1)} %fusion.66, f32[128,128,128]{2,0,1:T(8,128)S(1)} %fusion.64, f32[128,128]{1,0:T(8,128)S(1)} %copy.26, f32[128,128]{1,0:T(8,128)S(1)} %copy.25, ...), kind=kOutput, calls=%fused_computation.36 | convolution fusion | flops 1625407488 | bytes 33783808 | tf_op jit(solution)/shard_map/rcb,bd->rcd/dot_general | solution.py:25
  616.2 0.0 copy-start
  616.2 15.8 %fusion.32 = f32[128,128,128]{2,1,0:T(8,128)S(1)} fusion(f32[128,128,64]{1,2,0:T(8,128)} %add_multiply_fusion, f32[128,64]{0,1:T(8,128)S(1)} %get-tuple-element.19), kind=kOutput, calls=%fused_computation.41 | convolution fusion | flops 1611776000 | bytes 12615680 | tf_op jit(solution)/shard_map/rcd,bd->rcb/dot_general | solution.py:25
  632.0 0.0 copy-done
  632.0 15.7 %fusion.34 = f32[128,128,128]{2,1,0:T(8,128)} fusion(f32[128,128,64]{1,2,0:T(8,128)S(1)} %copy-done, f32[128,64]{0,1:T(8,128)S(1)} %get-tuple-element.19), kind=kOutput, calls=%fused_computation.43 | convolution fusion | flops 1611776000 | bytes 12615680 | tf_op jit(solution)/shard_map/rcd,bd->rcb/dot_general | solution.py:25
  647.7 15.9 %fusion.28 = f32[128,128,128]{2,1,0:T(8,128)} fusion(f32[128,128,64]{1,2,0:T(8,128)S(1)} %copy-done, f32[128,64]{0,1:T(8,128)S(1)} %get-tuple-element.17), kind=kOutput, calls=%fused_computation.37 | convolution fusion | flops 1611776000 | bytes 12615680 | tf_op jit(solution)/shard_map/rcd,bd->rcb/dot_general | solution.py:25
  663.6 15.6 %fusion.30 = f32[128,128,128]{2,1,0:T(8,128)} fusion(f32[128,128,64]{1,2,0:T(8,128)S(1)} %copy-done, f32[128,64]{0,1:T(8,128)S(1)} %get-tuple-element.17), kind=kOutput, calls=%fused_computation.39 | convolution fusion | flops 1611776000 | bytes 12615680 | tf_op jit(solution)/shard_map/rcd,bd->rcb/dot_general | solution.py:25
  679.2 12.9 %fusion.12 = f32[64,128,128]{2,0,1:T(8,128)} fusion(f32[128,128]{1,0:T(8,128)S(1)} %copy.26, f32[128,128]{1,0:T(8,128)S(1)} %copy.25, f32[128,128,128]{2,1,0:T(8,128)S(1)} %fusion.32, f32[128,128,128]{2,1,0:T(8,128)} %fusion.28, f32[128,128,128]{2,1,0:T(8,128)} %fusion.34, f32[128,128,128]{2,1,0:T(8,128)} %fusion.30, f32[128,128]{0,1:T(8,128)S(1)} %fusion.94), kind=kOutput, calls=%fused_computation.15 | convolution fusion | flops 1621098496 | bytes 37912576 | tf_op jit(solution)/shard_map/rcb,ca->rab/dot_general | solution.py:25
  692.1 0.0 copy-start.5
  692.1 0.0 copy-start.4
  692.1 14.0 %subtract_convert_fusion.1 = bf16[64,128,128]{2,0,1:T(8,128)(2,1)} fusion(f32[64,128,128]{2,0,1:T(8,128)} %fusion.12, f32[128,128]{1,0:T(8,128)S(1)} %copy.26, f32[128,128]{1,0:T(8,128)S(1)} %copy.25, f32[128,128,128]{2,1,0:T(8,128)S(1)} %fusion.32, f32[128,128,128]{2,1,0:T(8,128)} %fusion.28, f32[128,128,128]{2,1,0:T(8,128)} %fusion.34, ...), kind=kOutput, calls=%fused_computation.31 | convolution fusion | flops 1623195648 | bytes 40009728 | tf_op jit(solution)/shard_map/rcb,ca->rab/dot_general | solution.py:25
  706.1 4.7 copy.38
  710.8 0.0 all-gather.2.cloned.1.call-update
  710.9 0.0 copy-done.5
  710.9 0.0 copy-done.4
  710.9 0.1 convert_element_type.140
  711.0 1.4 multiply_cosine_fusion.1
  712.4 0.4 subtract_convert_fusion.2
  712.8 8.8 multiply_cosine_fusion
  721.6 138.1 %all-gather.2.cloned.1.call-done = bf16[512,8192]{1,0:T(8,128)(2,1)} async-done(((bf16[128,8192]{1,0:T(8,128)(2,1)}), bf16[512,8192]{1,0:T(8,128)(2,1)}) %all-gather.2.cloned.1.call-update) | async-done | bytes 8388624 | tf_op jit(solution)/shard_map/all_gather | solution.py:113
  859.7 5.2 fusion.153
  864.9 0.0 copy-start.2
  864.9 0.0 copy-start.3
  864.9 1.0 convert.18
  865.9 0.6 copy-done.2
  866.5 0.6 copy-done.3
  867.1 2.1 subtract_convert_fusion
  869.2 21.3 %multiply_reduce_fusion = (f32[2,768]{1,0:T(2,128)S(1)}, f32[2,768,8192]{2,1,0:T(8,128)}) fusion(bf16[2,64,8192]{2,1,0:T(8,128)(2,1)} %get-tuple-element.6, bf16[2,64,8192]{2,1,0:T(8,128)(2,1)S(1)} %get-tuple-element.5, bf16[2,768,64]{2,1,0:T(8,128)(2,1)S(1)} %get-tuple-element.10, bf16[2,768,64]{2,1,0:T(8,128)(2,1)S(1)} %get-tuple-element.9), kind=kOutput, calls=%fused_computation.1 | convolution fusion | flops 3255564800 | bytes 54925312 | tf_op jit(solution)/shard_map/hqd,hdn->hqn/dot_general | solution.py:126
  890.5 20.5 %fusion = f32[2,768]{1,0:T(2,128)S(1)} fusion(f32[2,768,8192]{2,1,0:T(8,128)} %get-tuple-element.23, f32[2,768]{1,0:T(2,128)S(1)} %get-tuple-element.22), kind=kLoop, calls=%fused_computation.2 | loop fusion | flops 37747200 | bytes 50343936 | tf_op jit(solution)/shard_map/reduce_sum | solution.py:132
  911.0 20.7 %fusion.54 = bf16[2,768,128]{2,1,0:T(8,128)(2,1)} fusion(bf16[2,128,8192]{2,1,0:T(8,128)(2,1)} %bitcast.82, f32[2,768,8192]{2,1,0:T(8,128)} %get-tuple-element.23, f32[2,768]{1,0:T(2,128)S(1)} %get-tuple-element.22, f32[2,768]{1,0:T(2,128)S(1)} %get-tuple-element.14, f32[2,768]{1,0:T(2,128)S(1)} %get-tuple-element.13), kind=kOutput, calls=%fused_computation.58 | convolution fusion | flops 3259564032 | bytes 54937600 | tf_op jit(solution)/shard_map/hqn,hdn->hqd/dot_general | solution.py:133
  (5 shorter events, 0.0 us)
Async XLA Ops:
  10.6 54.5 %all-to-all-start = ((bf16[4096,4,64]{0,2,1:T(8,128)(2,1)}), bf16[4096,4,64]{0,2,1:T(8,128)(2,1)S(1)}, u32[]{:S(2)}, u32[]{:S(2)}) async-start(bf16[4096,4,64]{0,2,1:T(8,128)(2,1)} %bitcast.79), calls=%async_computation | async-start | bytes 4194304 | tf_op jit(solution)/shard_map/all_to_all | solution.py:102
  65.2 52.3 %all-to-all-start.1 = ((bf16[4096,4,64]{0,2,1:T(8,128)(2,1)}), bf16[4096,4,64]{0,2,1:T(8,128)(2,1)}, u32[]{:S(2)}, u32[]{:S(2)}) async-start(bf16[4096,4,64]{0,2,1:T(8,128)(2,1)} %bitcast.77), calls=%async_computation.1 | async-start | bytes 4194304 | tf_op jit(solution)/shard_map/all_to_all | solution.py:103
  69.6 790.1 %all-gather.2.cloned.1.call-start = ((), (), s32[]{:S(2)}) async-start(), calls=%async_computation.2 | async-start | bytes 10485760 | tf_op jit(solution)/shard_map/all_gather | solution.py:113
  542.3 3.2 copy-start.1
  616.2 15.8 %copy-start = (f32[128,128,64]{1,2,0:T(8,128)S(1)}, f32[128,128,64]{1,2,0:T(8,128)}, u32[]{:S(2)}) copy-start(f32[128,128,64]{1,2,0:T(8,128)} %add_multiply_fusion) | copy-start | bytes 12582916
  692.1 18.8 %copy-start.5 = (s32[768]{0:T(1024)S(1)}, s32[768]{0:T(1024)}, u32[]{:S(2)}) copy-start(s32[768]{0:T(1024)} %param.7) | copy-start | bytes 9220
  692.1 18.8 %copy-start.4 = (bf16[2,768,128]{2,1,0:T(8,128)(2,1)S(1)}, bf16[2,768,128]{2,1,0:T(8,128)(2,1)}, u32[]{:S(2)}) copy-start(bf16[2,768,128]{2,1,0:T(8,128)(2,1)} %param.6) | copy-start | bytes 1179652
  864.9 1.6 copy-start.2
  864.9 2.2 copy-start.3
Sparse Core Ops, SparseCore 0:
  711.0 148.7 all-gather.1
where the time goes:
time: 949 us; the launch traced here: 939 us
  local copies, waits for them, and re-layouts  436 us (46%)
  waiting for transfers between devices  227 us (24%)
  matrix products  203 us (21%)
  other arithmetic  48.8 us (5%)
  between operations  14 us (1%)
  starting transfers between devices  10.8 us (1%)
    slice x1, local copies, waits for them, and re-layouts, compress(): signal[:, 1::2][:, ::-1]  185 us
    slice x1, local copies, waits for them, and re-layouts, compress(): signal[:, 0::2]  185 us
    dot_general x12, matrix products, contract(): return jnp.einsum(form, left, right, precision=highest)  161 us
    all_gather x1, waiting for transfers between devices, on_device(): whole = lax.all_gather(compact, 'ctx', axis=0, tiled=True)  138 us
    all_to_all x1, waiting for transfers between devices, on_device(): lax.all_to_all(values, 'ctx', split_axis=1, concat_axis=0, tiled=True)  44.7 us
    all_to_all x1, waiting for transfers between devices, on_device(): lax.all_to_all(keys, 'ctx', split_axis=1, concat_axis=0, tiled=True)  44.1 us
    rev x1, local copies, waits for them, and re-layouts, compress(): signal[:, 1::2][:, ::-1]  34.6 us
    unnamed x16, local copies, waits for them, and re-layouts  22.2 us
  transfers between devices with their start and end apart: 3, of which 3 were waited for; matrix products, arithmetic and copies ran while one was open for 2% of the time, Pallas kernels for 0%

commit v1 on v0

v1 whole, which is shorter than its diff:
```python
import functools
import math

import jax
import jax.numpy as jnp
import numpy as np
from jax import lax
from jax.experimental import pallas as pl
from jax.experimental.pallas import tpu as pltpu
from jax.sharding import PartitionSpec as P

OUTER = 128


def split_two(matrix):
    high = matrix.astype(jnp.bfloat16)
    low = (matrix - np.asarray(high).astype(np.float64)).astype(jnp.bfloat16)
    return high, low


@functools.lru_cache(maxsize=None)
def stages(length):
    outer = OUTER
    inner = length // outer
    step = inner // 2
    a = np.arange(outer)
    c = np.arange(outer)
    turn = 2 * outer
    angle = np.pi / outer * ((c[:, None] * a[None, :]) % turn)
    alternate = np.where(a % 2 == 0, 1.0, -1.0)
    first = np.stack([np.cos(angle), -np.sin(angle)], axis=1)
    first[0, 1] = alternate
    d = np.arange(length // 2 // turn)
    k = np.concatenate([c[:, None] + turn * d, (turn - c[:, None]) % turn + turn * d], axis=1)
    k[0, d.size :] = outer + turn * d
    sign = np.concatenate([np.ones(d.size), -np.ones(d.size)])
    b = np.arange(inner)
    q = np.arange(step)
    theta = np.pi / (2 * length) * ((k[:, :, None] * (2 * b + 1)) % (4 * length))
    phi = np.pi / length * ((k[:, None, :] * (2 * q + 1)[:, None]) % (2 * length))
    forward = np.stack([np.cos(theta), np.sin(theta) * sign[None, :, None]], axis=2)
    weight = np.where(k == 0, 1.0, 2.0) / length
    back = np.stack([np.cos(phi), np.sin(phi) * sign], axis=1) * weight[:, None, None, :]
    half = d.size
    forward[0, :half, 1] = 0.0
    forward[0, half:, 1] = np.cos(theta[0, half:])
    forward[0, half:, 0] = 0.0
    back[0, 1, :, :half] = 0.0
    back[0, 1, :, half:] = np.cos(phi[0, :, half:]) * weight[0, half:]
    back[0, 0, :, half:] = 0.0
    middle = back.reshape(outer, 2 * step, 2 * half) @ forward.reshape(outer, 2 * half, 2 * inner)
    last = first.transpose(2, 0, 1).reshape(outer, 2 * outer)
    return first.reshape(2 * outer, outer), middle, last


def compress(signal):
    length, columns = signal.shape
    outer, inner = OUTER, length // OUTER
    first, middle, last = stages(length)
    first_high, first_low = split_two(first)
    flat = signal.reshape(outer, inner * columns)
    one = jnp.dot(first_high, flat, preferred_element_type=jnp.float32) + jnp.dot(
        first_low, flat, preferred_element_type=jnp.float32
    )
    one = one.reshape(outer, 2 * inner, columns)
    two = jnp.einsum(
        "cob,cbl->col", jnp.asarray(middle.astype(np.float32)), one, precision=lax.Precision.HIGH
    )
    three = jnp.dot(
        jnp.asarray(last.astype(np.float32)),
        two.reshape(2 * outer, inner // 2 * columns),
        precision=lax.Precision.HIGH,
    )
    return three.reshape(length // 2, columns).astype(jnp.bfloat16)


def inverse_freq(width):
    return jnp.exp(jnp.arange(width // 2).astype(jnp.float32) * (-2.0 * math.log(500000.0) / width))


def rotate_rows(block, places):
    width = block.shape[-1]
    half = width // 2
    angles = places[:, None] * inverse_freq(width)[None, :]
    cosine = jnp.cos(angles)
    sine = jnp.sin(angles)
    first = block[..., :half]
    second = block[..., half:]
    return jnp.concatenate(
        [first * cosine - second * sine, second * cosine + first * sine], axis=-1
    )


def attend_kernel(chunk, scale, q_ref, k_ref, v_ref, out_ref, lse_ref):
    q = q_ref[0]
    rows, width = q.shape
    factor = scale * math.log2(math.e)
    best = jnp.full((rows, 1), -jnp.inf, jnp.float32)
    total = jnp.zeros((rows, 1), jnp.float32)
    accum = jnp.zeros((rows, width), jnp.float32)
    tokens = k_ref.shape[1]
    for start in range(0, tokens, chunk):
        k = k_ref[0, start : start + chunk, :]
        v = v_ref[0, start : start + chunk, :]
        scores = lax.dot_general(
            q, k, (((1,), (1,)), ((), ())), preferred_element_type=jnp.float32
        )
        fresh = jnp.maximum(best, jnp.max(scores, axis=1, keepdims=True))
        expo = jnp.exp2((scores - fresh) * factor)
        shrink = jnp.exp2((best - fresh) * factor)
        total = total * shrink + jnp.sum(expo, axis=1, keepdims=True)
        accum = accum * shrink + jnp.dot(
            expo.astype(jnp.bfloat16), v, preferred_element_type=jnp.float32
        )
        best = fresh
    out_ref[0] = (accum / total).astype(out_ref.dtype)
    lse_ref[0] = jnp.broadcast_to(best * factor + jnp.log2(total), (rows, 8))


def attend(queries, keys, values):
    groups, rows, width = queries.shape
    heads, tokens, _ = keys.shape
    per_head = groups // heads
    block = math.gcd(rows, 256)
    chunk = math.gcd(tokens, 1024)
    scale = 1.0 / math.sqrt(width)
    return pl.pallas_call(
        functools.partial(attend_kernel, chunk, scale),
        grid=(groups, rows // block),
        in_specs=[
            pl.BlockSpec((1, block, width), lambda g, i: (g, i, 0)),
            pl.BlockSpec((1, tokens, width), lambda g, i: (g // per_head, 0, 0)),
            pl.BlockSpec((1, tokens, width), lambda g, i: (g // per_head, 0, 0)),
        ],
        out_specs=[
            pl.BlockSpec((1, block, width), lambda g, i: (g, i, 0)),
            pl.BlockSpec((1, block, 8), lambda g, i: (g, i, 0)),
        ],
        out_shape=[
            jax.ShapeDtypeStruct((groups, rows, width), jnp.bfloat16),
            jax.ShapeDtypeStruct((groups, rows, 8), jnp.float32),
        ],
        cost_estimate=pl.CostEstimate(
            flops=4 * groups * rows * tokens * width,
            bytes_accessed=2 * groups * rows * width * 2,
            transcendentals=groups * rows * tokens,
        ),
    )(queries, keys, values)


def by_pairs(keys, values, queries, positions, count):
    heads, rows, width = queries.shape
    me = lax.axis_index("ctx")
    odd = me % 2 == 1
    pieces = []
    for head in range(heads):
        pieces.append(keys[:, head * width : (head + 1) * width])
        pieces.append(values[:, head * width : (head + 1) * width])
    mine = lax.all_to_all(jnp.stack(pieces), "ctx", split_axis=0, concat_axis=0, tiled=True)
    rotated = rotate_rows(queries.astype(jnp.float32), positions.astype(jnp.float32)).astype(
        jnp.bfloat16
    )
    asked = lax.all_to_all(
        jnp.repeat(rotated, 2, axis=0), "ctx", split_axis=0, concat_axis=0, tiled=True
    )
    compact = compress(mine.reshape(-1, width))
    tokens = compact.shape[0]
    half = tokens // 2
    low, high = compact[:half], compact[half:]
    places = (jnp.arange(half) + jnp.where(odd, half, 0)).astype(jnp.float32)
    other = lax.ppermute(
        jnp.where(odd, low, high), "ctx", [(i, i ^ 1) for i in range(count)]
    )
    key_rows = jnp.where(odd, other, low)
    value_rows = jnp.where(odd, high, other)
    ready = rotate_rows(key_rows.astype(jnp.float32), places).astype(jnp.bfloat16)
    part, lse = attend(asked, ready[None], value_rows[None])
    lse = lse[:, :, 0].reshape(count, rows // width, width)
    top = lax.reduce_precision(lse, 8, 7)
    rest = lse - top
    mid = lax.reduce_precision(rest, 8, 7)
    last = (rest - mid).astype(jnp.bfloat16)
    top, mid = top.astype(jnp.bfloat16), mid.astype(jnp.bfloat16)
    sent = lax.all_to_all(
        jnp.concatenate([part, top, mid, last], axis=1),
        "ctx",
        split_axis=0,
        concat_axis=0,
        tiled=True,
    )
    got = sent[:, :rows].astype(jnp.float32).reshape(heads, 2, rows, width)
    logs = jnp.sum(
        sent[:, rows:].astype(jnp.float32).reshape(heads, 2, 3, rows), axis=2
    )
    share = jax.nn.sigmoid((logs[:, 0] - logs[:, 1]) * math.log(2.0))[..., None]
    return (got[:, 0] * share + got[:, 1] * (1.0 - share)).astype(jnp.bfloat16)


def by_columns(keys, values, queries, positions):
    key_parts = lax.all_to_all(keys, "ctx", split_axis=1, concat_axis=0, tiled=True)
    value_parts = lax.all_to_all(values, "ctx", split_axis=1, concat_axis=0, tiled=True)
    heads, rows, width = queries.shape
    per_device = key_parts.shape[1]
    compact = compress(jnp.concatenate([key_parts, value_parts], axis=1))
    rotated = rotate_rows(queries.astype(jnp.float32), positions.astype(jnp.float32)).astype(
        jnp.bfloat16
    )
    whole = lax.all_gather(compact.T, "ctx", axis=0, tiled=True)
    tokens = whole.shape[1]
    shaped = whole.reshape(-1, 2, per_device, tokens)
    key_rows = shaped[:, 0].reshape(heads, width, tokens).swapaxes(1, 2)
    value_rows = shaped[:, 1].reshape(heads, width, tokens).swapaxes(1, 2)
    places = jnp.arange(tokens).astype(jnp.float32)
    ready = rotate_rows(key_rows.astype(jnp.float32), places).astype(jnp.bfloat16)
    return attend(rotated, ready, value_rows)[0]


def solution(mesh):
    count = mesh.shape["ctx"]

    def on_device(keys, values, queries, positions):
        heads, rows, width = queries.shape
        if count == 2 * heads and rows % width == 0:
            return by_pairs(keys, values, queries, positions, count)
        return by_columns(keys, values, queries, positions)

    return jax.shard_map(
        on_device,
        mesh=mesh,
        in_specs=(
            P(("user", "ctx"), "heads"),
            P(("user", "ctx"), "heads"),
            P("heads", ("user", "ctx"), None),
            P(("user", "ctx")),
        ),
        out_specs=P("heads", ("user", "ctx"), None),
        check_vma=False,
    )
```

time: 949 us -> 296 us (0.31)
  local copies, waits for them, and re-layouts: 436 us -> 58.8 us
  matrix products: 203 us -> 37.9 us
  waiting for transfers between devices: 227 us -> 121 us
  other arithmetic: 48.8 us -> 19.7 us
  Pallas kernels: 0 us -> 26.7 us
  blocking collectives: 0 us -> 19.6 us
  between operations: 14 us -> 0.21 us
    slice x3 -> x5, local copies, waits for them, and re-layouts: 376 us -> 3.14 us  [the longest x1 1.89 us: by_pairs(): lse = lse[:, :, 0].reshape(count, rows // width, width)]
    dot_general x14 -> x4, matrix products: 203 us -> 37.9 us  [the longest x1 17 us: compress(): jnp.einsum('cob,cbl->col', jnp.asarray(middle.astype(np.float32)), one, p...]
    all_gather x1 -> x0, waiting for transfers between devices: 138 us -> none  [on_device(): whole = lax.all_gather(compact, 'ctx', axis=0, tiled=True)]
    rev x1 -> x0, local copies, waits for them, and re-layouts: 34.6 us -> none  [compress(): signal[:, 1::2][:, ::-1]]
    reshape x0 -> x3, local copies, waits for them, and re-layouts: none -> 27.4 us  [the longest x1 18 us: compress(): one = one.reshape(outer, 2 * inner, columns)]
    ppermute x0 -> x1, waiting for transfers between devices: none -> 27.3 us  [by_pairs(): lax.ppermute(jnp.where(odd, low, high), 'ctx', [(i, i ^ 1) for i in range...]
    pallas_call x0 -> x1, Pallas kernels: none -> 26.7 us  [attend(): pl.pallas_call(functools.partial(attend_kernel, chunk, scale), grid=(grou...]
    unnamed x16 -> x11, local copies, waits for them, and re-layouts: 22.2 us -> 0.03 us
  transfers between devices with their start and end apart: 3 -> 3, of which waited for: 3 -> 2; matrix products, arithmetic and copies ran while one was open for 2% -> 5% of each run, Pallas kernels for 0% -> 0%
where the time goes in v1:
time: 296 us; the launch traced here: 294 us
  waiting for transfers between devices  121 us (41%)
  local copies, waits for them, and re-layouts  58.8 us (20%)
  matrix products  37.9 us (13%)
  Pallas kernels  26.7 us (9%)
  other arithmetic  19.7 us (7%)
  blocking collectives  19.6 us (7%)
  starting transfers between devices  10.5 us (4%)
    all_to_all x1, waiting for transfers between devices, by_pairs(): lax.all_to_all(jnp.stack(pieces), 'ctx', split_axis=0, concat_axis=0, til...  93.4 us
    ppermute x1, waiting for transfers between devices, by_pairs(): lax.ppermute(jnp.where(odd, low, high), 'ctx', [(i, i ^ 1) for i in range...  27.3 us
    pallas_call x1, Pallas kernels, attend(): pl.pallas_call(functools.partial(attend_kernel, chunk, scale), grid=(grou...  26.7 us
    all_to_all x1, blocking collectives, by_pairs(): lax.all_to_all(jnp.concatenate([part, top, mid, last], axis=1), 'ctx', sp...  19.6 us
    reshape x1, local copies, waits for them, and re-layouts, compress(): one = one.reshape(outer, 2 * inner, columns)  18 us
    add x1, local copies, waits for them, and re-layouts, compress(): jnp.dot(first_high, flat, preferred_element_type=jnp.float32)  17.5 us
    dot_general x1, matrix products, compress(): jnp.einsum('cob,cbl->col', jnp.asarray(middle.astype(np.float32)), one, p...  17 us
    concatenate x3, other arithmetic, rotate_rows(): jnp.concatenate([first * cosine - second * sine, second * cosine + first...  10.7 us
  transfers between devices with their start and end apart: 3, of which 2 were waited for; matrix products, arithmetic and copies ran while one was open for 5% of the time, Pallas kernels for 0%

profile of v1, /device:TPU:0, one launch (start us, length us, event | category | flops | bytes accessed | tf_op | source)
XLA Modules:
  0.0 294.2 jit_solution(17328774262737543508)
XLA Ops:
  0.0 2.4 slice_bitcast_fusion.2
  2.4 2.3 pad_maximum_fusion
  4.7 6.3 %all-to-all-start.1 = ((bf16[4,4096,128]{2,1,0:T(8,128)(2,1)}), bf16[4,4096,128]{2,1,0:T(8,128)(2,1)}, u32[]{:S(2)}, u32[]{:S(2)}) async-start(bf16[4,4096,128]{2,1,0:T(8,128)(2,1)} %pad_maximum_fusion), calls=%async_computation.1 | async-start | bytes 8388608 | tf_op jit(solution)/shard_map/all_to_all | solution.py:159
  11.1 0.0 copy-start.2
  11.1 93.4 %all-to-all-done.1 = bf16[4,4096,128]{2,1,0:T(8,128)(2,1)} async-done(((bf16[4,4096,128]{2,1,0:T(8,128)(2,1)}), bf16[4,4096,128]{2,1,0:T(8,128)(2,1)}, u32[]{:S(2)}, u32[]{:S(2)}) %all-to-all-start.1) | async-done | bytes 4194336 | tf_op jit(solution)/shard_map/all_to_all | solution.py:159
  104.5 7.3 %reshape_reshape.3 = bf16[128,16384]{1,0:T(8,128)(2,1)} reshape(bf16[4,4096,128]{2,1,0:T(8,128)(2,1)} %all-to-all-done.1) | data formatting | bytes 8388608 | tf_op jit(solution)/shard_map/reshape;reshape | solution.py:61
  111.8 0.0 copy-done.2
  111.8 0.0 copy-start.3
  111.8 4.6 %fusion.19 = f32[16384,256]{1,0:T(8,128)S(1)} fusion(bf16[128,16384]{1,0:T(8,128)(2,1)} %reshape_reshape.3, bf16[256,128]{1,0:T(8,128)(2,1)S(1)} %copy-done.2), kind=kOutput, calls=%fused_computation.52 | convolution fusion | flops 1073741824 | bytes 21037056 | tf_op jit(solution)/shard_map/dot_general | solution.py:62
  116.4 0.0 copy-done.3
  116.4 10.5 %fusion = f32[256,16384]{0,1:T(8,128)} fusion(f32[16384,256]{1,0:T(8,128)S(1)} %fusion.19, bf16[128,16384]{1,0:T(8,128)(2,1)} %reshape_reshape.3, bf16[256,128]{1,0:T(8,128)(2,1)S(1)} %copy-done.3), kind=kOutput, calls=%fused_computation.1 | convolution fusion | flops 1077936128 | bytes 37814272 | tf_op jit(solution)/shard_map/dot_general | solution.py:62
  126.9 17.5 %copy.14 = f32[256,16384]{1,0:T(8,128)} copy(f32[256,16384]{0,1:T(8,128)} %fusion) | data formatting | bytes 33554432 | tf_op jit(solution)/shard_map/add | solution.py:62
  144.3 18.0 %reshape.146 = f32[128,256,128]{2,1,0:T(8,128)} reshape(f32[256,16384]{1,0:T(8,128)} %copy.14) | data formatting | bytes 33554432 | tf_op jit(solution)/shard_map/reshape | solution.py:65
  162.3 17.0 %fusion.20 = f32[128,128,128]{2,1,0:T(8,128)} fusion(f32[128,128,256]{2,1,0:T(8,128)} %constant.40.clone, f32[128,256,128]{2,1,0:T(8,128)} %reshape.146), kind=kOutput, calls=%fused_computation.53 | convolution fusion | flops 3221225472 | bytes 41943040 | tf_op jit(solution)/shard_map/cob,cbl->col/dot_general | solution.py:66
  179.4 0.0 copy-start.1
  179.4 9.4 %reshape.147 = f32[256,8192]{1,0:T(8,128)} reshape(f32[128,128,128]{2,1,0:T(8,128)} %fusion.20) | data formatting | bytes 16777216 | tf_op jit(solution)/shard_map/reshape | solution.py:71
  188.8 0.0 copy-done.1
  188.8 5.7 %fusion.1 = bf16[128,8192]{1,0:T(8,128)(2,1)S(1)} fusion(f32[256,8192]{1,0:T(8,128)} %reshape.147, f32[128,256]{1,0:T(8,128)S(1)} %copy-done.1), kind=kOutput, calls=%fused_computation.3 | convolution fusion | flops 1611661312 | bytes 10616832 | tf_op jit(solution)/shard_map/dot_general | solution.py:69
  194.5 0.1 fusion.18
  194.7 0.0 copy-start.4
  194.7 0.0 copy-start
  194.7 0.5 slice.64
  195.2 0.5 slice.66
  195.8 1.1 broadcast_select_fusion
  196.8 0.0 collective-permute-start
  196.8 0.0 copy-done.4
  196.9 0.0 copy-done
  196.9 0.1 convert_element_type.56
  196.9 1.4 multiply_cosine_fusion.1
  198.4 0.4 subtract_convert_fusion
  198.8 0.2 pad_maximum_fusion.3
  199.0 1.0 broadcast_in_dim.4
  200.0 4.2 %all-to-all-start = ((bf16[4,768,128]{2,1,0:T(8,128)(2,1)}), bf16[4,768,128]{2,1,0:T(8,128)(2,1)}, u32[]{:S(2)}, u32[]{:S(2)}) async-start(bf16[4,768,128]{2,1,0:T(8,128)(2,1)} %bitcast), calls=%async_computation | async-start | bytes 1572864 | tf_op jit(solution)/shard_map/all_to_all | solution.py:163
  204.2 27.3 %collective-permute-done = bf16[4096,128]{1,0:T(8,128)(2,1)S(1)} collective-permute-done((bf16[4096,128]{1,0:T(8,128)(2,1)}, bf16[4096,128]{1,0:T(8,128)(2,1)S(1)}, u32[]{:S(2)}, u32[]{:S(2)}) %collective-permute-start) | collective-permute-done | bytes 1048608 | tf_op jit(solution)/shard_map/ppermute | solution.py:171
  231.5 1.2 select_bitcast_fusion
  232.7 8.9 %fusion.11 = (bf16[1,4096,64]{2,1,0:T(8,128)(2,1)S(1)}, bf16[1,4096,64]{2,1,0:T(8,128)(2,1)S(1)}) fusion(f32[4096,128]{1,0:T(8,128)S(1)} %get-tuple-element.20, f32[64]{0:T(128)S(1)} %multiply_exponential_fusion, f32[4096]{0:T(1024)S(1)} %add_convert_fusion.1), kind=kLoop, calls=%fused_computation.24 | loop fusion | flops 2359296 | bytes 3162368 | tf_op jit(solution)/shard_map/concatenate | solution.py:89
  241.6 1.6 pad_maximum_fusion.1.k_ref
  243.2 0.0 all-to-all-done.q_ref
  243.2 26.7 %shard_map.82 = (bf16[4,768,128]{2,1,0:T(8,128)(2,1)}, f32[4,768,8]{2,1,0:T(8,128)}) custom-call(bf16[4,768,128]{2,1,0:T(8,128)(2,1)} %all-to-all-done.q_ref, bf16[1,4096,128]{2,1,0:T(8,128)(2,1)} %pad_maximum_fusion.1.k_ref, bf16[1,4096,128]{2,1,0:T(8,128)(2,1)} %get-tuple-element.19.v_ref), custom_call_target="tpu_custom_call" | custom-call | flops 6442450944 | bytes 1572864 | tf_op jit(solution)/shard_map/pallas_call | solution.py:127
  269.9 1.9 slice_reduce_fusion
  271.8 1.2 pad_maximum_fusion.2
  273.0 19.6 %all_to_all.15 = bf16[4,786,128]{2,1,0:T(8,128)(2,1)S(1)} all-to-all(bf16[4,786,128]{2,1,0:T(8,128)(2,1)S(1)} %pad_maximum_fusion.2), channel_id=1, replica_groups=mesh['user'=4,'heads'=2,'ctx'=4] {'ctx'}, dimensions={0} | all-to-all | bytes 1609728 | tf_op jit(solution)/shard_map/all_to_all | solution.py:184
  292.8 0.1 slice.82
  292.9 0.1 convert.20
  293.0 1.2 fusion.14
  (11 shorter events, 0.1 us)
Async XLA Ops:
  4.7 99.8 %all-to-all-start.1 = ((bf16[4,4096,128]{2,1,0:T(8,128)(2,1)}), bf16[4,4096,128]{2,1,0:T(8,128)(2,1)}, u32[]{:S(2)}, u32[]{:S(2)}) async-start(bf16[4,4096,128]{2,1,0:T(8,128)(2,1)} %pad_maximum_fusion), calls=%async_computation.1 | async-start | bytes 8388608 | tf_op jit(solution)/shard_map/all_to_all | solution.py:159
  11.1 100.7 %copy-start.2 = (bf16[256,128]{1,0:T(8,128)(2,1)S(1)}, bf16[256,128]{1,0:T(8,128)(2,1)}, u32[]{:S(2)}) copy-start(bf16[256,128]{1,0:T(8,128)(2,1)} %constant.38.clone) | copy-start | bytes 196612
  111.8 4.6 %copy-start.3 = (bf16[256,128]{1,0:T(8,128)(2,1)S(1)}, bf16[256,128]{1,0:T(8,128)(2,1)}, u32[]{:S(2)}) copy-start(bf16[256,128]{1,0:T(8,128)(2,1)} %constant.39.clone) | copy-start | bytes 196612
  179.4 9.4 %copy-start.1 = (f32[128,256]{1,0:T(8,128)S(1)}, f32[128,256]{1,0:T(8,128)}, u32[]{:S(2)}) copy-start(f32[128,256]{1,0:T(8,128)} %constant.41.clone) | copy-start | bytes 393220
  194.7 2.2 copy-start.4
  194.7 2.2 copy-start
  196.8 34.7 %collective-permute-start = (bf16[4096,128]{1,0:T(8,128)(2,1)}, bf16[4096,128]{1,0:T(8,128)(2,1)S(1)}, u32[]{:S(2)}, u32[]{:S(2)}) collective-permute-start(bf16[4096,128]{1,0:T(8,128)(2,1)} %broadcast_select_fusion), channel_id=1, source_target_pairs={{0,1},{1,0},{2,3},{3,2},{4,5},{5,4},{6,7},{7,6},{8,9},{9,8},{10,11... | collective-permute-start | bytes 3145736 | tf_op jit(solution)/shard_map/ppermute | solution.py:171
  200.0 43.2 %all-to-all-start = ((bf16[4,768,128]{2,1,0:T(8,128)(2,1)}), bf16[4,768,128]{2,1,0:T(8,128)(2,1)}, u32[]{:S(2)}, u32[]{:S(2)}) async-start(bf16[4,768,128]{2,1,0:T(8,128)(2,1)} %bitcast), calls=%async_computation | async-start | bytes 1572864 | tf_op jit(solution)/shard_map/all_to_all | solution.py:163

commit v2 on v1

--- a/solution.py
+++ b/solution.py
@@ -73,6 +73,101 @@
     )
     return three.reshape(length // 2, columns).astype(jnp.bfloat16)
 
+GAP = 8
+
+
+def strict_dot(left_high, left_low, right):
+    high = right.astype(jnp.bfloat16)
+    low = (right - high.astype(jnp.float32)).astype(jnp.bfloat16)
+    dot = functools.partial(jnp.dot, preferred_element_type=jnp.float32)
+    return dot(left_high, high) + (dot(left_high, low) + dot(left_low, high))
+
+
+def compress_kernel(
+    inner, x_ref, first_ref, high_ref, low_ref, last_high_ref, last_low_ref, y_ref, wide_ref, one_ref
+):
+    outer = OUTER
+    step = inner // 2
+    here = pl.program_id(0)
+    steps = pl.num_programs(0)
+    per_step = high_ref.shape[0]
+    x_pitch = inner + GAP
+    one_pitch = 2 * outer + GAP
+    two_pitch = step + GAP
+
+    @pl.when(here == 0)
+    def _():
+        def widen(a, carry):
+            source = pl.multiple_of(a * inner, inner)
+            wide_ref[pl.ds(pl.multiple_of(a * x_pitch, GAP), inner), :] = x_ref[
+                pl.ds(source, inner), :
+            ].astype(jnp.float32)
+            return carry
+
+        lax.fori_loop(0, outer, widen, 0, unroll=2)
+
+        def stage_one(b, carry):
+            x = wide_ref[pl.ds(b, outer, stride=x_pitch), :].astype(jnp.bfloat16)
+            both = jnp.concatenate([x, x], axis=0)
+            one_ref[pl.ds(pl.multiple_of(b * one_pitch, GAP), 2 * outer), :] = jnp.dot(
+                first_ref[...], both, preferred_element_type=jnp.float32
+            )
+            return carry
+
+        lax.fori_loop(0, inner, stage_one, 0, unroll=4)
+
+    for i in range(per_step):
+        c = here * per_step + i
+        z = jnp.concatenate(
+            [
+                one_ref[pl.ds(2 * c, inner, stride=one_pitch), :],
+                one_ref[pl.ds(2 * c + 1, inner, stride=one_pitch), :],
+            ],
+            axis=0,
+        )
+        v = strict_dot(high_ref[i], low_ref[i], z)
+        for part in range(2):
+            wide_ref[pl.ds(pl.multiple_of((2 * c + part) * two_pitch, GAP), step), :] = v[
+                part * step : (part + 1) * step
+            ]
+
+    @pl.when(here == steps - 1)
+    def _():
+        def stage_three(q, carry):
+            v = wide_ref[pl.ds(q, 2 * outer, stride=two_pitch), :]
+            y = strict_dot(last_high_ref[...], last_low_ref[...], v)
+            y_ref[pl.ds(pl.multiple_of(q * outer, outer), outer), :] = y.astype(y_ref.dtype)
+            return carry
+
+        lax.fori_loop(0, step, stage_three, 0, unroll=4)
+
+
+def compress_rows(signal):
+    length, columns = signal.shape
+    outer, inner = OUTER, length // OUTER
+    first, middle, last = stages(length)
+    first_pair = np.concatenate(split_two(first), axis=1)
+    middle_high, middle_low = split_two(middle)
+    last_high, last_low = split_two(last)
+    per_step = 8
+    rows_wide = max(outer * (inner + GAP), 2 * outer * (inner // 2 + GAP))
+    once = pl.BlockSpec(memory_space=pltpu.VMEM)
+    block = pl.BlockSpec((per_step, inner, 2 * inner), lambda i: (i, 0, 0))
+    return pl.pallas_call(
+        functools.partial(compress_kernel, inner),
+        grid=(outer // per_step,),
+        in_specs=[once, once, block, block, once, once],
+        out_specs=once,
+        out_shape=jax.ShapeDtypeStruct((length // 2, columns), jnp.bfloat16),
+        scratch_shapes=[
+            pltpu.VMEM((rows_wide, columns), jnp.float32),
+            pltpu.VMEM((inner * (2 * outer + GAP), columns), jnp.float32),
+        ],
+        cost_estimate=pl.CostEstimate(
+            flops=16 * length * outer * columns, bytes_accessed=6 * length * columns, transcendentals=0
+        ),
+    )(signal, first_pair, middle_high, middle_low, last_high, last_low)
+
 
 def inverse_freq(width):
     return jnp.exp(jnp.arange(width // 2).astype(jnp.float32) * (-2.0 * math.log(500000.0) / width))
@@ -163,11 +258,12 @@
     asked = lax.all_to_all(
         jnp.repeat(rotated, 2, axis=0), "ctx", split_axis=0, concat_axis=0, tiled=True
     )
-    compact = compress(mine.reshape(-1, width))
+    compact = compress_rows(mine.reshape(-1, width))
     tokens = compact.shape[0]
     half = tokens // 2
     low, high = compact[:half], compact[half:]
-    places = (jnp.arange(half) + jnp.where(odd, half, 0)).astype(jnp.float32)
+    at = jnp.arange(half) + jnp.where(odd, half, 0)
+    places = (at % OUTER * (tokens // OUTER) + at // OUTER).astype(jnp.float32)
     other = lax.ppermute(
         jnp.where(odd, low, high), "ctx", [(i, i ^ 1) for i in range(count)]
     )

time: 296 us -> 239 us (0.81)
  local copies, waits for them, and re-layouts: 58.8 us -> 5.51 us
  matrix products: 37.9 us -> 0 us
  Pallas kernels: 26.7 us -> 61.1 us
    dot_general x4 -> x0, matrix products: 37.9 us -> none  [the longest x1 17 us: compress(): jnp.einsum('cob,cbl->col', jnp.asarray(middle.astype(np.float32)), one, p...]
    pallas_call x0 -> x1, Pallas kernels: none -> 34.4 us  [compress_rows(): pl.pallas_call(functools.partial(compress_kernel, inner), grid=(outer //...]
    reshape x2 -> x0, local copies, waits for them, and re-layouts: 27.4 us -> none  [the longest x1 18 us: compress(): one = one.reshape(outer, 2 * inner, columns)]
    add x1 -> x0, local copies, waits for them, and re-layouts: 17.5 us -> none  [compress(): jnp.dot(first_high, flat, preferred_element_type=jnp.float32)]
    another operation x1 -> x0, local copies, waits for them, and re-layouts: 7.29 us -> none  [compress(): flat = signal.reshape(outer, inner * columns)]
  transfers between devices with their start and end apart: 3 -> 3, of which waited for: 2 -> 2; matrix products, arithmetic and copies ran while one was open for 5% -> 6% of each run, Pallas kernels for 0% -> 0%
where the time goes in v2:
time: 239 us; the launch traced here: 238 us
  waiting for transfers between devices  121 us (51%)
  Pallas kernels  61.1 us (26%)
  other arithmetic  20.2 us (8%)
  blocking collectives  19.6 us (8%)
  starting transfers between devices  10.5 us (4%)
  local copies, waits for them, and re-layouts  5.51 us (2%)
    all_to_all x1, waiting for transfers between devices, by_pairs(): lax.all_to_all(jnp.stack(pieces), 'ctx', split_axis=0, concat_axis=0, til...  93.4 us
    pallas_call x1, Pallas kernels, compress_rows(): pl.pallas_call(functools.partial(compress_kernel, inner), grid=(outer //...  34.4 us
    ppermute x1, waiting for transfers between devices, by_pairs(): lax.ppermute(jnp.where(odd, low, high), 'ctx', [(i, i ^ 1) for i in range...  27.3 us
    pallas_call x1, Pallas kernels, attend(): pl.pallas_call(functools.partial(attend_kernel, chunk, scale), grid=(grou...  26.7 us
    all_to_all x1, blocking collectives, by_pairs(): lax.all_to_all(jnp.concatenate([part, top, mid, last], axis=1), 'ctx', sp...  19.6 us
    concatenate x3, other arithmetic, rotate_rows(): jnp.concatenate([first * cosine - second * sine, second * cosine + first...  10.7 us
    all_to_all x1, starting transfers between devices, by_pairs(): lax.all_to_all(jnp.stack(pieces), 'ctx', split_axis=0, concat_axis=0, til...  6.35 us
  transfers between devices with their start and end apart: 3, of which 2 were waited for; matrix products, arithmetic and copies ran while one was open for 6% of the time, Pallas kernels for 0%

profile of v2, /device:TPU:0, one launch (start us, length us, event | category | flops | bytes accessed | tf_op | source)
XLA Modules:
  0.0 237.9 jit_solution(3994459630058124576)
XLA Ops:
  0.0 2.4 %slice_bitcast_fusion.2 = (bf16[1,4096,128]{2,1,0:T(8,128)(2,1)S(1)}, bf16[1,4096,128]{2,1,0:T(8,128)(2,1)S(1)}, bf16[1,4096,128]{2,1,0:T(8,128)(2,1)S(1)}, bf16[1,4096,128]{2,1,0:T(8,128)(2,1)S(1)}) fusion(bf16[4096,256]{1,0:T(8,128)(2,1)} %param.10, bf16[4096,256]{1,0:T(8,128)(2,1)} %param.9), kind=kLoop, calls=%fused_computation.17 | loop fusion | bytes 8388608 | tf_op jit(solution)/shard_map/stack | solution.py:254
  2.4 2.3 pad_maximum_fusion
  4.7 6.3 %all-to-all-start.1 = ((bf16[4,4096,128]{2,1,0:T(8,128)(2,1)}), bf16[4,4096,128]{2,1,0:T(8,128)(2,1)}, u32[]{:S(2)}, u32[]{:S(2)}) async-start(bf16[4,4096,128]{2,1,0:T(8,128)(2,1)} %pad_maximum_fusion), calls=%async_computation.1 | async-start | bytes 8388608 | tf_op jit(solution)/shard_map/all_to_all | solution.py:254
  11.1 93.4 %all-to-all-done.1 = bf16[4,4096,128]{2,1,0:T(8,128)(2,1)} async-done(((bf16[4,4096,128]{2,1,0:T(8,128)(2,1)}), bf16[4,4096,128]{2,1,0:T(8,128)(2,1)}, u32[]{:S(2)}, u32[]{:S(2)}) %all-to-all-start.1) | async-done | bytes 4194336 | tf_op jit(solution)/shard_map/all_to_all | solution.py:254
  104.5 34.4 %shard_map.91 = bf16[8192,128]{1,0:T(8,128)(2,1)} custom-call(bf16[16384,128]{1,0:T(8,128)(2,1)} %bitcast.5.x_ref, bf16[256,256]{1,0:T(8,128)(2,1)} %constant.68.clone.first_ref, bf16[128,128,256]{2,1,0:T(8,128)(2,1)} %constant.69.clone.high_ref, bf16[128,128,256]{2,1,0:T(8,128)(2,1)} %constant.70.clone.low_ref, ...), custom_call_target="tpu_custom_call" | custom-call | flops 4294967296 | bytes 12582912 | tf_op jit(solution)/shard_map/pallas_call | solution.py:156
  138.9 0.0 copy-start.3
  138.9 0.0 copy-start.2
  138.9 2.7 %broadcast_select_fusion = bf16[4096,128]{1,0:T(8,128)(2,1)} fusion(pred[]{:T(512)S(6)} %eq.7, bf16[8192,128]{1,0:T(8,128)(2,1)} %shard_map.91), kind=kLoop, calls=%fused_computation.21 | loop fusion | flops 524288 | bytes 3145729 | tf_op jit(solution)/shard_map/jit(_where)/select_n | solution.py:268
  141.6 0.0 collective-permute-start
  141.6 0.0 copy-done.3
  141.6 0.0 copy-done.2
  141.6 0.1 convert_element_type.49
  141.7 1.4 multiply_cosine_fusion.1
  143.1 0.4 subtract_convert_fusion
  143.5 0.0 copy-start
  143.5 0.2 pad_maximum_fusion.3
  143.7 1.0 broadcast_in_dim.4
  144.8 4.2 %all-to-all-start = ((bf16[4,768,128]{2,1,0:T(8,128)(2,1)}), bf16[4,768,128]{2,1,0:T(8,128)(2,1)}, u32[]{:S(2)}, u32[]{:S(2)}) async-start(bf16[4,768,128]{2,1,0:T(8,128)(2,1)} %bitcast), calls=%async_computation | async-start | bytes 1572864 | tf_op jit(solution)/shard_map/all_to_all | solution.py:258
  149.0 27.3 %collective-permute-done = bf16[4096,128]{1,0:T(8,128)(2,1)S(1)} collective-permute-done((bf16[4096,128]{1,0:T(8,128)(2,1)}, bf16[4096,128]{1,0:T(8,128)(2,1)S(1)}, u32[]{:S(2)}, u32[]{:S(2)}) %collective-permute-start) | collective-permute-done | bytes 1048608 | tf_op jit(solution)/shard_map/ppermute | solution.py:267
  176.3 0.0 copy-done
  176.3 1.2 select_bitcast_fusion
  177.4 8.9 %fusion.9 = (bf16[1,4096,64]{2,1,0:T(8,128)(2,1)S(1)}, bf16[1,4096,64]{2,1,0:T(8,128)(2,1)S(1)}) fusion(f32[4096,128]{1,0:T(8,128)S(1)} %get-tuple-element.10, f32[64]{0:T(128)S(1)} %multiply_exponential_fusion, f32[4096]{0:T(1024)S(1)} %fusion.17), kind=kLoop, calls=%fused_computation.20 | loop fusion | flops 2359296 | bytes 3162368 | tf_op jit(solution)/shard_map/concatenate | solution.py:184
  186.4 1.6 pad_maximum_fusion.1.k_ref
  187.9 0.0 all-to-all-done.q_ref
  188.0 26.7 %shard_map.92 = (bf16[4,768,128]{2,1,0:T(8,128)(2,1)}, f32[4,768,8]{2,1,0:T(8,128)}) custom-call(bf16[4,768,128]{2,1,0:T(8,128)(2,1)} %all-to-all-done.q_ref, bf16[1,4096,128]{2,1,0:T(8,128)(2,1)} %pad_maximum_fusion.1.k_ref, bf16[1,4096,128]{2,1,0:T(8,128)(2,1)} %get-tuple-element.9.v_ref), custom_call_target="tpu_custom_call" | custom-call | flops 6442450944 | bytes 1572864 | tf_op jit(solution)/shard_map/pallas_call | solution.py:222
  214.7 0.0 copy-start.1
  214.7 2.0 slice_reduce_fusion
  216.7 0.0 copy-done.1
  216.7 0.1 pad_maximum_fusion.2
  216.7 19.6 %all_to_all.15 = bf16[4,786,128]{2,1,0:T(8,128)(2,1)S(1)} all-to-all(bf16[4,786,128]{2,1,0:T(8,128)(2,1)S(1)} %pad_maximum_fusion.2), channel_id=1, replica_groups=mesh['user'=4,'heads'=2,'ctx'=4] {'ctx'}, dimensions={0} | all-to-all | bytes 1609728 | tf_op jit(solution)/shard_map/all_to_all | solution.py:280
  236.5 0.1 slice.74
  236.6 0.1 convert.20
  236.7 1.2 fusion.12
  (11 shorter events, 0.2 us)
Async XLA Ops:
  4.7 99.8 %all-to-all-start.1 = ((bf16[4,4096,128]{2,1,0:T(8,128)(2,1)}), bf16[4,4096,128]{2,1,0:T(8,128)(2,1)}, u32[]{:S(2)}, u32[]{:S(2)}) async-start(bf16[4,4096,128]{2,1,0:T(8,128)(2,1)} %pad_maximum_fusion), calls=%async_computation.1 | async-start | bytes 8388608 | tf_op jit(solution)/shard_map/all_to_all | solution.py:254
  138.9 2.7 %copy-start.3 = (s32[768]{0:T(1024)S(1)}, s32[768]{0:T(1024)}, u32[]{:S(2)}) copy-start(s32[768]{0:T(1024)} %param.12) | copy-start | bytes 9220
  138.9 2.7 %copy-start.2 = (bf16[2,768,128]{2,1,0:T(8,128)(2,1)S(1)}, bf16[2,768,128]{2,1,0:T(8,128)(2,1)}, u32[]{:S(2)}) copy-start(bf16[2,768,128]{2,1,0:T(8,128)(2,1)} %param.11) | copy-start | bytes 1179652
  141.6 34.7 %collective-permute-start = (bf16[4096,128]{1,0:T(8,128)(2,1)}, bf16[4096,128]{1,0:T(8,128)(2,1)S(1)}, u32[]{:S(2)}, u32[]{:S(2)}) collective-permute-start(bf16[4096,128]{1,0:T(8,128)(2,1)} %broadcast_select_fusion), channel_id=1, source_target_pairs={{0,1},{1,0},{2,3},{3,2},{4,5},{5,4},{6,7},{7,6},{8,9},{9,8},{10,11... | collective-permute-start | bytes 3145736 | tf_op jit(solution)/shard_map/ppermute | solution.py:267
  143.5 32.7 %copy-start = (bf16[8192,128]{1,0:T(8,128)(2,1)S(1)}, bf16[8192,128]{1,0:T(8,128)(2,1)}, u32[]{:S(2)}) copy-start(bf16[8192,128]{1,0:T(8,128)(2,1)} %shard_map.91) | copy-start | bytes 6291460
  144.8 43.2 %all-to-all-start = ((bf16[4,768,128]{2,1,0:T(8,128)(2,1)}), bf16[4,768,128]{2,1,0:T(8,128)(2,1)}, u32[]{:S(2)}, u32[]{:S(2)}) async-start(bf16[4,768,128]{2,1,0:T(8,128)(2,1)} %bitcast), calls=%async_computation | async-start | bytes 1572864 | tf_op jit(solution)/shard_map/all_to_all | solution.py:258
  214.7 2.0 copy-start.1

commit v3 on v2

--- a/solution.py
+++ b/solution.py
@@ -76,21 +76,36 @@
 GAP = 8
 
 
-def strict_dot(left_high, left_low, right):
+def strict_dot(left, right):
+    rows, columns = left.shape[0] // 2, right.shape[1]
     high = right.astype(jnp.bfloat16)
     low = (right - high.astype(jnp.float32)).astype(jnp.bfloat16)
-    dot = functools.partial(jnp.dot, preferred_element_type=jnp.float32)
-    return dot(left_high, high) + (dot(left_high, low) + dot(left_low, high))
+    both = jnp.dot(
+        left, jnp.concatenate([high, low], axis=1), preferred_element_type=jnp.float32
+    )
+    return both[:rows, :columns] + (both[:rows, columns:] + both[rows:, :columns])
 
 
 def compress_kernel(
-    inner, x_ref, first_ref, high_ref, low_ref, last_high_ref, last_low_ref, y_ref, wide_ref, one_ref
+    inner,
+    odd_ref,
+    x_ref,
+    first_ref,
+    middle_ref,
+    last_ref,
+    coarse_ref,
+    fine_ref,
+    keep_ref,
+    send_ref,
+    wide_ref,
+    one_ref,
 ):
     outer = OUTER
     step = inner // 2
+    columns = x_ref.shape[1]
     here = pl.program_id(0)
     steps = pl.num_programs(0)
-    per_step = high_ref.shape[0]
+    per_step = middle_ref.shape[0]
     x_pitch = inner + GAP
     one_pitch = 2 * outer + GAP
     two_pitch = step + GAP
@@ -104,17 +119,27 @@
             ].astype(jnp.float32)
             return carry
 
-        lax.fori_loop(0, outer, widen, 0, unroll=2)
-
-        def stage_one(b, carry):
-            x = wide_ref[pl.ds(b, outer, stride=x_pitch), :].astype(jnp.bfloat16)
-            both = jnp.concatenate([x, x], axis=0)
-            one_ref[pl.ds(pl.multiple_of(b * one_pitch, GAP), 2 * outer), :] = jnp.dot(
-                first_ref[...], both, preferred_element_type=jnp.float32
+        lax.fori_loop(0, outer, widen, 0, unroll=4)
+
+        def stage_one(pair, carry):
+            x = jnp.concatenate(
+                [
+                    wide_ref[pl.ds(2 * pair + i, outer, stride=x_pitch), :].astype(jnp.bfloat16)
+                    for i in range(2)
+                ],
+                axis=1,
             )
+            z = jnp.dot(
+                first_ref[...],
+                jnp.concatenate([x, x], axis=0),
+                preferred_element_type=jnp.float32,
+            )
+            for i in range(2):
+                start = pl.multiple_of((2 * pair + i) * one_pitch, GAP)
+                one_ref[pl.ds(start, 2 * outer), :] = z[:, i * columns : (i + 1) * columns]
             return carry
 
-        lax.fori_loop(0, inner, stage_one, 0, unroll=4)
+        lax.fori_loop(0, inner // 2, stage_one, 0, unroll=4)
 
     for i in range(per_step):
         c = here * per_step + i
@@ -125,7 +150,7 @@
             ],
             axis=0,
         )
-        v = strict_dot(high_ref[i], low_ref[i], z)
+        v = strict_dot(middle_ref[i], z)
         for part in range(2):
             wide_ref[pl.ds(pl.multiple_of((2 * c + part) * two_pitch, GAP), step), :] = v[
                 part * step : (part + 1) * step
@@ -133,40 +158,76 @@
 
     @pl.when(here == steps - 1)
     def _():
-        def stage_three(q, carry):
-            v = wide_ref[pl.ds(q, 2 * outer, stride=two_pitch), :]
-            y = strict_dot(last_high_ref[...], last_low_ref[...], v)
-            y_ref[pl.ds(pl.multiple_of(q * outer, outer), outer), :] = y.astype(y_ref.dtype)
-            return carry
-
-        lax.fori_loop(0, step, stage_three, 0, unroll=4)
-
-
-def compress_rows(signal):
+        def stage_three(out_ref, offset):
+            def one(i, carry):
+                q = offset + i
+                v = wide_ref[pl.ds(q, 2 * outer, stride=two_pitch), :]
+                y = strict_dot(last_ref[...], v).astype(jnp.bfloat16).astype(jnp.float32)
+                front = lax.broadcasted_iota(jnp.int32, y.shape, 1) < columns // 2
+                cos_p, sin_p = coarse_ref[0], coarse_ref[1]
+                cos_q, sin_q = fine_ref[0, pl.ds(q, 1), :], fine_ref[1, pl.ds(q, 1), :]
+                sine = sin_p * cos_q + cos_p * sin_q
+                other = pltpu.roll(y, columns // 2, 1)
+                turned = y * (cos_p * cos_q - sin_p * sin_q) + other * jnp.where(
+                    front, -sine, sine
+                )
+                out_ref[pl.ds(pl.multiple_of(i * outer, outer), outer), :] = turned.astype(
+                    out_ref.dtype
+                )
+                return carry
+
+            lax.fori_loop(0, step // 2, one, 0, unroll=4)
+
+        odd = odd_ref[0]
+        stage_three(send_ref, (1 - odd) * (step // 2))
+        stage_three(keep_ref, odd * (step // 2))
+
+
+def turns(places, width):
+    angles = places[:, None] * inverse_freq(width)[None, :]
+    cosine, sine = jnp.cos(angles), jnp.sin(angles)
+    return jnp.stack(
+        [jnp.concatenate([cosine, cosine], axis=1), jnp.concatenate([sine, sine], axis=1)]
+    )
+
+
+def compress_rows(signal, odd):
     length, columns = signal.shape
     outer, inner = OUTER, length // OUTER
+    step = inner // 2
     first, middle, last = stages(length)
     first_pair = np.concatenate(split_two(first), axis=1)
-    middle_high, middle_low = split_two(middle)
-    last_high, last_low = split_two(last)
+    middle_pair = np.concatenate(split_two(middle), axis=1)
+    last_pair = np.concatenate(split_two(last), axis=0)
+    turned = (1 - odd).astype(jnp.float32)
+    coarse = turns(jnp.arange(outer).astype(jnp.float32) * step * turned, columns)
+    fine = turns(jnp.arange(step).astype(jnp.float32) * turned, columns)
     per_step = 8
-    rows_wide = max(outer * (inner + GAP), 2 * outer * (inner // 2 + GAP))
+    rows_wide = max(outer * (inner + GAP), 2 * outer * (step + GAP))
     once = pl.BlockSpec(memory_space=pltpu.VMEM)
-    block = pl.BlockSpec((per_step, inner, 2 * inner), lambda i: (i, 0, 0))
+    half = jax.ShapeDtypeStruct((length // 4, columns), jnp.bfloat16)
     return pl.pallas_call(
         functools.partial(compress_kernel, inner),
         grid=(outer // per_step,),
-        in_specs=[once, once, block, block, once, once],
-        out_specs=once,
-        out_shape=jax.ShapeDtypeStruct((length // 2, columns), jnp.bfloat16),
+        in_specs=[
+            pl.BlockSpec(memory_space=pltpu.SMEM),
+            once,
+            once,
+            pl.BlockSpec((per_step, 2 * inner, 2 * inner), lambda i: (i, 0, 0)),
+            once,
+            once,
+            once,
+        ],
+        out_specs=[once, once],
+        out_shape=[half, half],
         scratch_shapes=[
             pltpu.VMEM((rows_wide, columns), jnp.float32),
             pltpu.VMEM((inner * (2 * outer + GAP), columns), jnp.float32),
         ],
         cost_estimate=pl.CostEstimate(
-            flops=16 * length * outer * columns, bytes_accessed=6 * length * columns, transcendentals=0
+            flops=64 * length * outer * columns, bytes_accessed=16 * length * columns, transcendentals=0
         ),
-    )(signal, first_pair, middle_high, middle_low, last_high, last_low)
+    )(odd.reshape(1), signal, first_pair, middle_pair, last_pair, coarse, fine)
 
 
 def inverse_freq(width):
@@ -186,8 +247,9 @@
     )
 
 
-def attend_kernel(chunk, scale, q_ref, k_ref, v_ref, out_ref, lse_ref):
+def attend_kernel(chunk, scale, swap_ref, q_ref, k_ref, v_ref, out_ref, lse_ref):
     q = q_ref[0]
+    swap = swap_ref[0] == 1
     rows, width = q.shape
     factor = scale * math.log2(math.e)
     best = jnp.full((rows, 1), -jnp.inf, jnp.float32)
@@ -195,8 +257,9 @@
     accum = jnp.zeros((rows, width), jnp.float32)
     tokens = k_ref.shape[1]
     for start in range(0, tokens, chunk):
-        k = k_ref[0, start : start + chunk, :]
-        v = v_ref[0, start : start + chunk, :]
+        one = k_ref[0, start : start + chunk, :]
+        two = v_ref[0, start : start + chunk, :]
+        k, v = jnp.where(swap, two, one), jnp.where(swap, one, two)
         scores = lax.dot_general(
             q, k, (((1,), (1,)), ((), ())), preferred_element_type=jnp.float32
         )
@@ -212,7 +275,7 @@
     lse_ref[0] = jnp.broadcast_to(best * factor + jnp.log2(total), (rows, 8))
 
 
-def attend(queries, keys, values):
+def attend(queries, keys, values, swap):
     groups, rows, width = queries.shape
     heads, tokens, _ = keys.shape
     per_head = groups // heads
@@ -223,6 +286,7 @@
         functools.partial(attend_kernel, chunk, scale),
         grid=(groups, rows // block),
         in_specs=[
+            pl.BlockSpec(memory_space=pltpu.SMEM),
             pl.BlockSpec((1, block, width), lambda g, i: (g, i, 0)),
             pl.BlockSpec((1, tokens, width), lambda g, i: (g // per_head, 0, 0)),
             pl.BlockSpec((1, tokens, width), lambda g, i: (g // per_head, 0, 0)),
@@ -240,13 +304,13 @@
             bytes_accessed=2 * groups * rows * width * 2,
             transcendentals=groups * rows * tokens,
         ),
-    )(queries, keys, values)
+    )(swap.reshape(1), queries, keys, values)
 
 
 def by_pairs(keys, values, queries, positions, count):
     heads, rows, width = queries.shape
     me = lax.axis_index("ctx")
-    odd = me % 2 == 1
+    odd = (me % 2).astype(jnp.int32)
     pieces = []
     for head in range(heads):
         pieces.append(keys[:, head * width : (head + 1) * width])
@@ -258,19 +322,9 @@
     asked = lax.all_to_all(
         jnp.repeat(rotated, 2, axis=0), "ctx", split_axis=0, concat_axis=0, tiled=True
     )
-    compact = compress_rows(mine.reshape(-1, width))
-    tokens = compact.shape[0]
-    half = tokens // 2
-    low, high = compact[:half], compact[half:]
-    at = jnp.arange(half) + jnp.where(odd, half, 0)
-    places = (at % OUTER * (tokens // OUTER) + at // OUTER).astype(jnp.float32)
-    other = lax.ppermute(
-        jnp.where(odd, low, high), "ctx", [(i, i ^ 1) for i in range(count)]
-    )
-    key_rows = jnp.where(odd, other, low)
-    value_rows = jnp.where(odd, high, other)
-    ready = rotate_rows(key_rows.astype(jnp.float32), places).astype(jnp.bfloat16)
-    part, lse = attend(asked, ready[None], value_rows[None])
+    keep, send = compress_rows(mine.reshape(-1, width), odd)
+    other = lax.ppermute(send, "ctx", [(i, i ^ 1) for i in range(count)])
+    part, lse = attend(asked, keep[None], other[None], odd)
     lse = lse[:, :, 0].reshape(count, rows // width, width)
     top = lax.reduce_precision(lse, 8, 7)
     rest = lse - top
@@ -308,7 +362,7 @@
     value_rows = shaped[:, 1].reshape(heads, width, tokens).swapaxes(1, 2)
     places = jnp.arange(tokens).astype(jnp.float32)
     ready = rotate_rows(key_rows.astype(jnp.float32), places).astype(jnp.bfloat16)
-    return attend(rotated, ready, value_rows)[0]
+    return attend(rotated, ready, value_rows, jnp.zeros((), jnp.int32))[0]
 
 
 def solution(mesh):

time: 239 us -> 220 us (0.921)
  other arithmetic: 20.2 us -> 7.81 us
  waiting for transfers between devices: 121 us -> 112 us
  blocking collectives: 19.6 us -> 23.2 us
  Pallas kernels: 61.1 us -> 58.2 us
    concatenate x3 -> x1, other arithmetic: 10.7 us -> 0.22 us  [rotate_rows(): jnp.concatenate([first * cosine - second * sine, second * cosine + first...]
    ppermute x1, waiting for transfers between devices: 27.3 us -> 22.3 us  [by_pairs(): other = lax.ppermute(send, 'ctx', [(i, i ^ 1) for i in range(count)])]
    pallas_call x1, Pallas kernels: 34.4 us -> 29.9 us  [compress_rows(): pl.pallas_call(functools.partial(compress_kernel, inner), grid=(outer //...]
    all_to_all x1, waiting for transfers between devices: 93.4 us -> 89.2 us  [by_pairs(): lax.all_to_all(jnp.stack(pieces), 'ctx', split_axis=0, concat_axis=0, til...]
    all_to_all x1, blocking collectives: 19.6 us -> 23.2 us  [by_pairs(): lax.all_to_all(jnp.concatenate([part, top, mid, last], axis=1), 'ctx', sp...]
    select_n x1 -> x0, other arithmetic: 2.68 us -> none  [by_pairs(): jnp.where(odd, low, high)]
  transfers between devices with their start and end apart: 3 -> 3, of which waited for: 2 -> 2; matrix products, arithmetic and copies ran while one was open for 6% -> 2% of each run, Pallas kernels for 0% -> 14%
where the time goes in v3:
time: 220 us; the launch traced here: 219 us
  waiting for transfers between devices  112 us (51%)
  Pallas kernels  58.2 us (26%)
  blocking collectives  23.2 us (11%)
  starting transfers between devices  11.9 us (5%)
  other arithmetic  7.81 us (4%)
  local copies, waits for them, and re-layouts  6.49 us (3%)
    all_to_all x1, waiting for transfers between devices, by_pairs(): lax.all_to_all(jnp.stack(pieces), 'ctx', split_axis=0, concat_axis=0, til...  89.2 us
    pallas_call x1, Pallas kernels, compress_rows(): pl.pallas_call(functools.partial(compress_kernel, inner), grid=(outer //...  29.9 us
    pallas_call x1, Pallas kernels, attend(): pl.pallas_call(functools.partial(attend_kernel, chunk, scale), grid=(grou...  28.3 us
    all_to_all x1, blocking collectives, by_pairs(): lax.all_to_all(jnp.concatenate([part, top, mid, last], axis=1), 'ctx', sp...  23.2 us
    ppermute x1, waiting for transfers between devices, by_pairs(): other = lax.ppermute(send, 'ctx', [(i, i ^ 1) for i in range(count)])  22.3 us
    all_to_all x1, starting transfers between devices, by_pairs(): lax.all_to_all(jnp.stack(pieces), 'ctx', split_axis=0, concat_axis=0, til...  6.48 us
  transfers between devices with their start and end apart: 3, of which 2 were waited for; matrix products, arithmetic and copies ran while one was open for 2% of the time, Pallas kernels for 14%

profile of v3, /device:TPU:0, one launch (start us, length us, event | category | flops | bytes accessed | tf_op | source)
XLA Modules:
  0.0 219.4 jit_solution(578838968230101587)
XLA Ops:
  0.0 2.4 %slice_bitcast_fusion.2 = (bf16[1,4096,128]{2,1,0:T(8,128)(2,1)S(1)}, bf16[1,4096,128]{2,1,0:T(8,128)(2,1)S(1)}, bf16[1,4096,128]{2,1,0:T(8,128)(2,1)S(1)}, bf16[1,4096,128]{2,1,0:T(8,128)(2,1)S(1)}) fusion(bf16[4096,256]{1,0:T(8,128)(2,1)} %param.8, bf16[4096,256]{1,0:T(8,128)(2,1)} %param.7), kind=kLoop, calls=%fused_computation.4 | loop fusion | bytes 8388608 | tf_op jit(solution)/shard_map/stack | solution.py:318
  2.4 2.2 %pad_maximum_fusion = bf16[4,4096,128]{2,1,0:T(8,128)(2,1)} fusion(bf16[1,4096,128]{2,1,0:T(8,128)(2,1)S(1)} %get-tuple-element.16, bf16[1,4096,128]{2,1,0:T(8,128)(2,1)S(1)} %get-tuple-element.28, bf16[1,4096,128]{2,1,0:T(8,128)(2,1)S(1)} %get-tuple-element.15, bf16[1,4096,128]{2,1,0:T(8,128)(2,1)S(1)} %get-tuple-element.29), kind=kLoop, calls=%fused_computation | loop fusion | flops 6291456 | bytes 8388608 | tf_op jit(solution)/shard_map/stack | solution.py:318
  4.7 0.0 copy-start.3
  4.7 0.0 copy-start.2
  4.7 6.5 %all-to-all-start.1 = ((bf16[4,4096,128]{2,1,0:T(8,128)(2,1)}), bf16[4,4096,128]{2,1,0:T(8,128)(2,1)}, u32[]{:S(2)}, u32[]{:S(2)}) async-start(bf16[4,4096,128]{2,1,0:T(8,128)(2,1)} %pad_maximum_fusion), calls=%async_computation.1 | async-start | bytes 8388608 | tf_op jit(solution)/shard_map/all_to_all | solution.py:318
  11.2 0.0 copy-done.3
  11.2 0.0 copy-done.2
  11.2 0.1 convert_element_type.51
  11.3 0.2 multiply_cosine_fusion.2
  11.5 0.1 maximum_bitcast_fusion.2
  11.6 0.6 pad_maximum_fusion.4.fine_ref
  12.2 0.3 multiply_cosine_fusion.1
  12.5 0.1 maximum_bitcast_fusion
  12.6 0.7 pad_maximum_fusion.3.coarse_ref
  13.3 1.4 multiply_cosine_fusion
  14.7 0.4 subtract_convert_fusion
  15.1 0.2 pad_maximum_fusion.2
  15.3 89.2 %all-to-all-done.1 = bf16[4,4096,128]{2,1,0:T(8,128)(2,1)} async-done(((bf16[4,4096,128]{2,1,0:T(8,128)(2,1)}), bf16[4,4096,128]{2,1,0:T(8,128)(2,1)}, u32[]{:S(2)}, u32[]{:S(2)}) %all-to-all-start.1) | async-done | bytes 4194336 | tf_op jit(solution)/shard_map/all_to_all | solution.py:318
  104.6 1.0 broadcast_in_dim.6
  105.6 3.5 %all-to-all-start = ((bf16[4,768,128]{2,1,0:T(8,128)(2,1)}), bf16[4,768,128]{2,1,0:T(8,128)(2,1)S(1)}, u32[]{:S(2)}, u32[]{:S(2)}) async-start(bf16[4,768,128]{2,1,0:T(8,128)(2,1)} %bitcast.1), calls=%async_computation | async-start | bytes 1572864 | tf_op jit(solution)/shard_map/all_to_all | solution.py:322
  109.1 29.9 %shard_map.73 = (bf16[4096,128]{1,0:T(8,128)(2,1)}, bf16[4096,128]{1,0:T(8,128)(2,1)}) custom-call(s32[1]{0:T(128)} %bitcast.odd_ref.swap_ref, bf16[16384,128]{1,0:T(8,128)(2,1)} %bitcast.6.x_ref, bf16[256,256]{1,0:T(8,128)(2,1)} %constant.35.clone.first_ref, bf16[128,256,256]{2,1,0:T(8,128)(2,1)} %constant.36.clone.middle_ref, ...), custom_call_target="tpu_custom_call" | custom-call | flops 17179869184 | bytes 33554432 | tf_op jit(solution)/shard_map/pallas_call | solution.py:209
  139.0 2.0 collective-permute-start
  141.0 0.0 all-to-all-done.q_ref
  141.0 0.0 copy-start
  141.0 22.3 %collective-permute-done = bf16[4096,128]{1,0:T(8,128)(2,1)S(1)} collective-permute-done((bf16[4096,128]{1,0:T(8,128)(2,1)}, bf16[4096,128]{1,0:T(8,128)(2,1)S(1)}, u32[]{:S(2)}, u32[]{:S(2)}) %collective-permute-start) | collective-permute-done | bytes 1048608 | tf_op jit(solution)/shard_map/ppermute | solution.py:326
  163.3 0.0 copy-start.4
  163.3 0.0 copy-done
  163.3 1.0 copy-done.4
  164.2 28.3 %shard_map.74 = (bf16[4,768,128]{2,1,0:T(8,128)(2,1)}, f32[4,768,8]{2,1,0:T(8,128)}) custom-call(s32[1]{0:T(128)} %bitcast.odd_ref.swap_ref, bf16[4,768,128]{2,1,0:T(8,128)(2,1)} %copy-done, bf16[1,4096,128]{2,1,0:T(8,128)(2,1)} %bitcast.49, bf16[1,4096,128]{2,1,0:T(8,128)(2,1)} %bitcast.48), custom_call_target="tpu_custom_call" | custom-call | flops 6442450944 | bytes 1572864 | tf_op jit(solution)/shard_map/pallas_call | solution.py:285
  192.6 0.0 copy-start.1
  192.6 2.0 slice_reduce_fusion
  194.6 0.0 copy-done.1
  194.6 0.1 pad_maximum_fusion.1
  194.7 23.2 %all_to_all.15 = bf16[4,786,128]{2,1,0:T(8,128)(2,1)S(1)} all-to-all(bf16[4,786,128]{2,1,0:T(8,128)(2,1)S(1)} %pad_maximum_fusion.1), channel_id=1, replica_groups=mesh['user'=4,'heads'=2,'ctx'=4] {'ctx'}, dimensions={0} | all-to-all | bytes 1609728 | tf_op jit(solution)/shard_map/all_to_all | solution.py:334
  218.0 0.1 slice.54
  218.1 0.1 convert.10
  218.2 1.2 fusion.2
  (12 shorter events, 0.1 us)
Async XLA Ops:
  4.7 6.5 %copy-start.3 = (s32[768]{0:T(1024)S(1)}, s32[768]{0:T(1024)}, u32[]{:S(2)}) copy-start(s32[768]{0:T(1024)} %param.10) | copy-start | bytes 9220
  4.7 6.5 %copy-start.2 = (bf16[2,768,128]{2,1,0:T(8,128)(2,1)S(1)}, bf16[2,768,128]{2,1,0:T(8,128)(2,1)}, u32[]{:S(2)}) copy-start(bf16[2,768,128]{2,1,0:T(8,128)(2,1)} %param.9) | copy-start | bytes 1179652
  4.7 99.9 %all-to-all-start.1 = ((bf16[4,4096,128]{2,1,0:T(8,128)(2,1)}), bf16[4,4096,128]{2,1,0:T(8,128)(2,1)}, u32[]{:S(2)}, u32[]{:S(2)}) async-start(bf16[4,4096,128]{2,1,0:T(8,128)(2,1)} %pad_maximum_fusion), calls=%async_computation.1 | async-start | bytes 8388608 | tf_op jit(solution)/shard_map/all_to_all | solution.py:318
  105.6 35.4 %all-to-all-start = ((bf16[4,768,128]{2,1,0:T(8,128)(2,1)}), bf16[4,768,128]{2,1,0:T(8,128)(2,1)S(1)}, u32[]{:S(2)}, u32[]{:S(2)}) async-start(bf16[4,768,128]{2,1,0:T(8,128)(2,1)} %bitcast.1), calls=%async_computation | async-start | bytes 1572864 | tf_op jit(solution)/shard_map/all_to_all | solution.py:322
  139.0 24.3 %collective-permute-start = (bf16[4096,128]{1,0:T(8,128)(2,1)}, bf16[4096,128]{1,0:T(8,128)(2,1)S(1)}, u32[]{:S(2)}, u32[]{:S(2)}) collective-permute-start(bf16[4096,128]{1,0:T(8,128)(2,1)} %get-tuple-element.10), channel_id=1, source_target_pairs={{0,1},{1,0},{2,3},{3,2},{4,5},{5,4},{6,7},{7,6},{8,9},{9,8},{10,11... | collective-permute-start | bytes 3145736 | tf_op jit(solution)/shard_map/ppermute | solution.py:326
  141.0 22.3 %copy-start = (bf16[4,768,128]{2,1,0:T(8,128)(2,1)}, bf16[4,768,128]{2,1,0:T(8,128)(2,1)S(1)}, u32[]{:S(2)}) copy-start(bf16[4,768,128]{2,1,0:T(8,128)(2,1)S(1)} %all-to-all-done.q_ref) | copy-start | bytes 2359300
  163.3 1.0 copy-start.4
  192.6 2.0 copy-start.1

commit v4 on v3

--- a/solution.py
+++ b/solution.py
@@ -96,7 +96,8 @@
     coarse_ref,
     fine_ref,
     keep_ref,
-    send_ref,
+    send_one_ref,
+    send_two_ref,
     wide_ref,
     one_ref,
 ):
@@ -176,10 +177,11 @@
                 )
                 return carry
 
-            lax.fori_loop(0, step // 2, one, 0, unroll=4)
+            lax.fori_loop(0, out_ref.shape[0] // outer, one, 0, unroll=4)
 
         odd = odd_ref[0]
-        stage_three(send_ref, (1 - odd) * (step // 2))
+        stage_three(send_one_ref, (1 - odd) * (step // 2))
+        stage_three(send_two_ref, (1 - odd) * (step // 2) + step // 4)
         stage_three(keep_ref, odd * (step // 2))
 
 
@@ -206,6 +208,7 @@
     rows_wide = max(outer * (inner + GAP), 2 * outer * (step + GAP))
     once = pl.BlockSpec(memory_space=pltpu.VMEM)
     half = jax.ShapeDtypeStruct((length // 4, columns), jnp.bfloat16)
+    quarter = jax.ShapeDtypeStruct((length // 8, columns), jnp.bfloat16)
     return pl.pallas_call(
         functools.partial(compress_kernel, inner),
         grid=(outer // per_step,),
@@ -218,8 +221,8 @@
             once,
             once,
         ],
-        out_specs=[once, once],
-        out_shape=[half, half],
+        out_specs=[once, once, once],
+        out_shape=[half, quarter, quarter],
         scratch_shapes=[
             pltpu.VMEM((rows_wide, columns), jnp.float32),
             pltpu.VMEM((inner * (2 * outer + GAP), columns), jnp.float32),
@@ -247,14 +250,20 @@
     )
 
 
-def attend_kernel(chunk, scale, swap_ref, q_ref, k_ref, v_ref, out_ref, lse_ref):
+def attend_kernel(chunk, scale, resume, finish, swap_ref, q_ref, k_ref, v_ref, *refs):
     q = q_ref[0]
     swap = swap_ref[0] == 1
     rows, width = q.shape
     factor = scale * math.log2(math.e)
-    best = jnp.full((rows, 1), -jnp.inf, jnp.float32)
-    total = jnp.zeros((rows, 1), jnp.float32)
-    accum = jnp.zeros((rows, width), jnp.float32)
+    if resume:
+        accum = refs[0][0]
+        best = refs[1][0][:, :1]
+        total = refs[2][0][:, :1]
+        refs = refs[3:]
+    else:
+        best = jnp.full((rows, 1), -jnp.inf, jnp.float32)
+        total = jnp.zeros((rows, 1), jnp.float32)
+        accum = jnp.zeros((rows, width), jnp.float32)
     tokens = k_ref.shape[1]
     for start in range(0, tokens, chunk):
         one = k_ref[0, start : start + chunk, :]
@@ -271,60 +280,91 @@
             expo.astype(jnp.bfloat16), v, preferred_element_type=jnp.float32
         )
         best = fresh
-    out_ref[0] = (accum / total).astype(out_ref.dtype)
-    lse_ref[0] = jnp.broadcast_to(best * factor + jnp.log2(total), (rows, 8))
-
-
-def attend(queries, keys, values, swap):
+    if finish:
+        refs[0][0] = (accum / total).astype(refs[0].dtype)
+        refs[1][0] = jnp.broadcast_to(best * factor + jnp.log2(total), (rows, 8))
+    else:
+        refs[0][0] = accum
+        refs[1][0] = jnp.broadcast_to(best, (rows, 8))
+        refs[2][0] = jnp.broadcast_to(total, (rows, 8))
+
+
+def attend(queries, keys, values, swap, part=0, parts=1, state=None):
     groups, rows, width = queries.shape
-    heads, tokens, _ = keys.shape
+    heads, tokens, _ = values.shape
     per_head = groups // heads
     block = math.gcd(rows, 256)
     chunk = math.gcd(tokens, 1024)
     scale = 1.0 / math.sqrt(width)
+    finish = part == parts - 1
+    wide = pl.BlockSpec((1, block, width), lambda g, i: (g, i, 0))
+    thin = pl.BlockSpec((1, block, 8), lambda g, i: (g, i, 0))
+    thin_shape = jax.ShapeDtypeStruct((groups, rows, 8), jnp.float32)
+    state = () if state is None else tuple(state)
+    wide_type = jnp.bfloat16 if finish else jnp.float32
     return pl.pallas_call(
-        functools.partial(attend_kernel, chunk, scale),
+        functools.partial(attend_kernel, chunk, scale, bool(state), finish),
         grid=(groups, rows // block),
         in_specs=[
             pl.BlockSpec(memory_space=pltpu.SMEM),
-            pl.BlockSpec((1, block, width), lambda g, i: (g, i, 0)),
+            wide,
+            pl.BlockSpec((1, tokens, width), lambda g, i: (g // per_head, part, 0)),
             pl.BlockSpec((1, tokens, width), lambda g, i: (g // per_head, 0, 0)),
-            pl.BlockSpec((1, tokens, width), lambda g, i: (g // per_head, 0, 0)),
-        ],
-        out_specs=[
-            pl.BlockSpec((1, block, width), lambda g, i: (g, i, 0)),
-            pl.BlockSpec((1, block, 8), lambda g, i: (g, i, 0)),
-        ],
-        out_shape=[
-            jax.ShapeDtypeStruct((groups, rows, width), jnp.bfloat16),
-            jax.ShapeDtypeStruct((groups, rows, 8), jnp.float32),
-        ],
+        ]
+        + ([wide, thin, thin] if state else []),
+        out_specs=[wide, thin] if finish else [wide, thin, thin],
+        out_shape=[jax.ShapeDtypeStruct((groups, rows, width), wide_type), thin_shape]
+        + ([] if finish else [thin_shape]),
         cost_estimate=pl.CostEstimate(
-            flops=4 * groups * rows * tokens * width,
-            bytes_accessed=2 * groups * rows * width * 2,
+            flops=8 * groups * rows * tokens * width,
+            bytes_accessed=4 * groups * rows * width * 2,
             transcendentals=groups * rows * tokens,
         ),
-    )(swap.reshape(1), queries, keys, values)
+    )(swap.reshape(1), queries, keys, values, *state)
+
+
+def stack_kernel(keys_ref, values_ref, out_ref):
+    width = out_ref.shape[2]
+    for head in range(out_ref.shape[0] // 2):
+        columns = slice(head * width, (head + 1) * width)
+        out_ref[2 * head] = keys_ref[:, columns]
+        out_ref[2 * head + 1] = values_ref[:, columns]
+
+
+def stack(keys, values, width):
+    rows, columns = keys.shape
+    pieces = 2 * columns // width
+    block = math.gcd(rows, 512)
+    spec = pl.BlockSpec((block, columns), lambda i: (i, 0))
+    return pl.pallas_call(
+        stack_kernel,
+        grid=(rows // block,),
+        in_specs=[spec, spec],
+        out_specs=pl.BlockSpec((pieces, block, width), lambda i: (0, i, 0)),
+        out_shape=jax.ShapeDtypeStruct((pieces, rows, width), keys.dtype),
+    )(keys, values)
 
 
 def by_pairs(keys, values, queries, positions, count):
     heads, rows, width = queries.shape
     me = lax.axis_index("ctx")
     odd = (me % 2).astype(jnp.int32)
-    pieces = []
-    for head in range(heads):
-        pieces.append(keys[:, head * width : (head + 1) * width])
-        pieces.append(values[:, head * width : (head + 1) * width])
-    mine = lax.all_to_all(jnp.stack(pieces), "ctx", split_axis=0, concat_axis=0, tiled=True)
+    mine = lax.all_to_all(
+        stack(keys, values, width), "ctx", split_axis=0, concat_axis=0, tiled=True
+    )
     rotated = rotate_rows(queries.astype(jnp.float32), positions.astype(jnp.float32)).astype(
         jnp.bfloat16
     )
     asked = lax.all_to_all(
         jnp.repeat(rotated, 2, axis=0), "ctx", split_axis=0, concat_axis=0, tiled=True
     )
-    keep, send = compress_rows(mine.reshape(-1, width), odd)
-    other = lax.ppermute(send, "ctx", [(i, i ^ 1) for i in range(count)])
-    part, lse = attend(asked, keep[None], other[None], odd)
+    keep, *sends = compress_rows(mine.reshape(-1, width), odd)
+    pairs = [(i, i ^ 1) for i in range(count)]
+    others = [lax.ppermute(send, "ctx", pairs) for send in sends]
+    state = None
+    for part, other in enumerate(others):
+        state = attend(asked, keep[None], other[None], odd, part, len(others), state)
+    part, lse = state
     lse = lse[:, :, 0].reshape(count, rows // width, width)
     top = lax.reduce_precision(lse, 8, 7)
     rest = lse - top

time: 220 us -> 220 us (level)
  Pallas kernels: 58.2 us -> 73.1 us
  waiting for transfers between devices: 112 us -> 102 us
  other arithmetic: 7.81 us -> 5.56 us
    pallas_call x1 -> x3, Pallas kernels: 28.3 us -> 43.3 us  [the longest x2 36.5 us: attend(): pl.pallas_call(functools.partial(attend_kernel, chunk, scale, bool(state)...]
    ppermute x1 -> x2, waiting for transfers between devices: 22.3 us -> 13 us  [by_pairs(): others = [lax.ppermute(send, 'ctx', pairs) for send in sends]]
    another operation x1 -> x0, local copies, waits for them, and re-layouts: 2.44 us -> none  [by_pairs(): jnp.stack(pieces)]
    another operation x2 -> x1, other arithmetic: 2.64 us -> 0.39 us  [the longest x1 2.25 us: by_pairs(): jnp.stack(pieces)]
  transfers between devices with their start and end apart: 3 -> 4, of which waited for: 2 -> 2; matrix products, arithmetic and copies ran while one was open for 2% -> 2% of each run, Pallas kernels for 14% -> 21%
where the time goes in v4:
time: 220 us; the launch traced here: 219 us
  waiting for transfers between devices  102 us (46%)
  Pallas kernels  73.1 us (33%)
  blocking collectives  21.2 us (10%)
  starting transfers between devices  12 us (5%)
  other arithmetic  5.56 us (3%)
  local copies, waits for them, and re-layouts  4.67 us (2%)
    all_to_all x1, waiting for transfers between devices, by_pairs(): lax.all_to_all(stack(keys, values, width), 'ctx', split_axis=0, concat_ax...  89.2 us
    pallas_call x2, Pallas kernels, attend(): pl.pallas_call(functools.partial(attend_kernel, chunk, scale, bool(state)...  36.5 us
    pallas_call x1, Pallas kernels, compress_rows(): pl.pallas_call(functools.partial(compress_kernel, inner), grid=(outer //...  29.9 us
    all_to_all x1, blocking collectives, by_pairs(): lax.all_to_all(jnp.concatenate([part, top, mid, last], axis=1), 'ctx', sp...  21.2 us
    ppermute x2, waiting for transfers between devices, by_pairs(): others = [lax.ppermute(send, 'ctx', pairs) for send in sends]  13 us
    pallas_call x1, Pallas kernels, stack(): pl.pallas_call(stack_kernel, grid=(rows // block,), in_specs=[spec, spec]...  6.77 us
    all_to_all x1, starting transfers between devices, by_pairs(): lax.all_to_all(stack(keys, values, width), 'ctx', split_axis=0, concat_ax...  6.48 us
  transfers between devices with their start and end apart: 4, of which 2 were waited for; matrix products, arithmetic and copies ran while one was open for 2% of the time, Pallas kernels for 21%

profile of v4, /device:TPU:0, one launch (start us, length us, event | category | flops | bytes accessed | tf_op | source)
XLA Modules:
  0.0 219.0 jit_solution(16720874439988582481)
XLA Ops:
  0.0 6.8 %shard_map.73 = bf16[4,4096,128]{2,1,0:T(8,128)(2,1)} custom-call(bf16[4096,256]{1,0:T(8,128)(2,1)} %keys_ref.1, bf16[4096,256]{1,0:T(8,128)(2,1)} %values_ref.1), custom_call_target="tpu_custom_call" | custom-call | tf_op jit(solution)/shard_map/pallas_call | solution.py:339
  6.8 0.0 copy-start.3
  6.8 0.0 copy-start.2
  6.8 6.5 %all-to-all-start.1 = ((bf16[4,4096,128]{2,1,0:T(8,128)(2,1)}), bf16[4,4096,128]{2,1,0:T(8,128)(2,1)}, u32[]{:S(2)}, u32[]{:S(2)}) async-start(bf16[4,4096,128]{2,1,0:T(8,128)(2,1)} %shard_map.73), calls=%async_computation.1 | async-start | bytes 8388608 | tf_op jit(solution)/shard_map/all_to_all | solution.py:352
  13.3 0.0 copy-done.3
  13.3 0.0 copy-done.2
  13.3 0.1 convert_element_type.51
  13.4 0.2 multiply_cosine_fusion.2
  13.6 0.1 maximum_bitcast_fusion.2
  13.7 0.6 pad_maximum_fusion.3.fine_ref
  14.3 0.3 multiply_cosine_fusion.1
  14.6 0.1 maximum_bitcast_fusion
  14.7 0.7 pad_maximum_fusion.2.coarse_ref
  15.4 1.4 multiply_cosine_fusion
  16.8 0.4 subtract_convert_fusion
  17.2 0.2 pad_maximum_fusion.1
  17.4 89.2 %all-to-all-done.1 = bf16[4,4096,128]{2,1,0:T(8,128)(2,1)} async-done(((bf16[4,4096,128]{2,1,0:T(8,128)(2,1)}), bf16[4,4096,128]{2,1,0:T(8,128)(2,1)}, u32[]{:S(2)}, u32[]{:S(2)}) %all-to-all-start.1) | async-done | bytes 4194336 | tf_op jit(solution)/shard_map/all_to_all | solution.py:352
  106.7 1.0 broadcast_in_dim.8
  107.7 3.5 %all-to-all-start = ((bf16[4,768,128]{2,1,0:T(8,128)(2,1)}), bf16[4,768,128]{2,1,0:T(8,128)(2,1)S(1)}, u32[]{:S(2)}, u32[]{:S(2)}) async-start(bf16[4,768,128]{2,1,0:T(8,128)(2,1)} %bitcast.1), calls=%async_computation | async-start | bytes 1572864 | tf_op jit(solution)/shard_map/all_to_all | solution.py:358
  111.2 29.9 %shard_map.74 = (bf16[4096,128]{1,0:T(8,128)(2,1)}, bf16[2048,128]{1,0:T(8,128)(2,1)}, bf16[2048,128]{1,0:T(8,128)(2,1)}) custom-call(s32[1]{0:T(128)} %bitcast.odd_ref.swap_ref, bf16[16384,128]{1,0:T(8,128)(2,1)} %bitcast.2.x_ref, bf16[256,256]{1,0:T(8,128)(2,1)} %constant.35.clone.first_ref, bf16[128,256,256]{2,1,0:T(8,128)(2,1)} %constant.36.clone.middle_ref, ...), custom_call_target="tpu_custom_call" | custom-call | flops 17179869184 | bytes 33554432 | tf_op jit(solution)/shard_map/pallas_call | solution.py:212
  141.0 2.0 collective-permute-start.1
  143.0 0.1 collective-permute-start
  143.1 0.0 all-to-all-done.q_ref
  143.1 0.0 copy-start
  143.1 13.0 %collective-permute-done.1 = bf16[2048,128]{1,0:T(8,128)(2,1)S(1)} collective-permute-done((bf16[2048,128]{1,0:T(8,128)(2,1)}, bf16[2048,128]{1,0:T(8,128)(2,1)S(1)}, u32[]{:S(2)}, u32[]{:S(2)}) %collective-permute-start.1) | collective-permute-done | bytes 524320 | tf_op jit(solution)/shard_map/ppermute | solution.py:363
  156.0 0.0 copy-start.5
  156.0 0.0 copy-done
  156.0 0.8 copy-done.5
  156.8 16.5 %shard_map.75 = (f32[4,768,128]{2,1,0:T(8,128)}, f32[4,768,8]{2,1,0:T(8,128)}, f32[4,768,8]{2,1,0:T(8,128)}) custom-call(s32[1]{0:T(128)} %bitcast.odd_ref.swap_ref, bf16[4,768,128]{2,1,0:T(8,128)(2,1)} %copy-done, bf16[1,4096,128]{2,1,0:T(8,128)(2,1)} %bitcast.43, bf16[1,2048,128]{2,1,0:T(8,128)(2,1)} %bitcast.42), custom_call_target="tpu_custom_call" | custom-call | flops 6442450944 | bytes 3145728 | tf_op jit(solution)/shard_map/pallas_call | solution.py:305
  173.3 0.0 collective-permute-done
  173.3 0.0 copy-start.4
  173.4 0.8 copy-done.4
  174.2 20.0 %shard_map.76 = (bf16[4,768,128]{2,1,0:T(8,128)(2,1)}, f32[4,768,8]{2,1,0:T(8,128)}) custom-call(s32[1]{0:T(128)} %bitcast.odd_ref.swap_ref, bf16[4,768,128]{2,1,0:T(8,128)(2,1)} %copy-done, bf16[1,4096,128]{2,1,0:T(8,128)(2,1)} %bitcast.44, bf16[1,2048,128]{2,1,0:T(8,128)(2,1)} %bitcast.41, f32[4,768,128]{2,1,0:T(8,128)} %get-tuple-element.16.refs_0_, ...), custom_call_target="tpu_custom_call" | custom-call | flops 6442450944 | bytes 3145728 | tf_op jit(solution)/shard_map/pallas_call | solution.py:305
  194.2 0.0 copy-start.1
  194.2 2.0 slice_reduce_fusion
  196.2 0.0 copy-done.1
  196.2 0.1 pad_maximum_fusion
  196.2 21.2 %all_to_all.15 = bf16[4,786,128]{2,1,0:T(8,128)(2,1)S(1)} all-to-all(bf16[4,786,128]{2,1,0:T(8,128)(2,1)S(1)} %pad_maximum_fusion), channel_id=1, replica_groups=mesh['user'=4,'heads'=2,'ctx'=4] {'ctx'}, dimensions={0} | all-to-all | bytes 1609728 | tf_op jit(solution)/shard_map/all_to_all | solution.py:374
  217.6 0.1 slice.38
  217.6 0.1 convert.10
  217.7 1.2 fusion.2
  (12 shorter events, 0.1 us)
Async XLA Ops:
  6.8 6.5 %copy-start.3 = (s32[768]{0:T(1024)S(1)}, s32[768]{0:T(1024)}, u32[]{:S(2)}) copy-start(s32[768]{0:T(1024)} %param.10) | copy-start | bytes 9220
  6.8 6.5 %copy-start.2 = (bf16[2,768,128]{2,1,0:T(8,128)(2,1)S(1)}, bf16[2,768,128]{2,1,0:T(8,128)(2,1)}, u32[]{:S(2)}) copy-start(bf16[2,768,128]{2,1,0:T(8,128)(2,1)} %param.9) | copy-start | bytes 1179652
  6.8 99.9 %all-to-all-start.1 = ((bf16[4,4096,128]{2,1,0:T(8,128)(2,1)}), bf16[4,4096,128]{2,1,0:T(8,128)(2,1)}, u32[]{:S(2)}, u32[]{:S(2)}) async-start(bf16[4,4096,128]{2,1,0:T(8,128)(2,1)} %shard_map.73), calls=%async_computation.1 | async-start | bytes 8388608 | tf_op jit(solution)/shard_map/all_to_all | solution.py:352
  107.7 35.4 %all-to-all-start = ((bf16[4,768,128]{2,1,0:T(8,128)(2,1)}), bf16[4,768,128]{2,1,0:T(8,128)(2,1)S(1)}, u32[]{:S(2)}, u32[]{:S(2)}) async-start(bf16[4,768,128]{2,1,0:T(8,128)(2,1)} %bitcast.1), calls=%async_computation | async-start | bytes 1572864 | tf_op jit(solution)/shard_map/all_to_all | solution.py:358
  141.0 15.0 %collective-permute-start.1 = (bf16[2048,128]{1,0:T(8,128)(2,1)}, bf16[2048,128]{1,0:T(8,128)(2,1)S(1)}, u32[]{:S(2)}, u32[]{:S(2)}) collective-permute-start(bf16[2048,128]{1,0:T(8,128)(2,1)} %get-tuple-element.15), channel_id=1, source_target_pairs={{0,1},{1,0},{2,3},{3,2},{4,5},{5,4},{6,7},{7,6},{8,9},{9,8},{10,11... | collective-permute-start | bytes 1572872 | tf_op jit(solution)/shard_map/ppermute | solution.py:363
  143.0 30.3 %collective-permute-start = (bf16[2048,128]{1,0:T(8,128)(2,1)}, bf16[2048,128]{1,0:T(8,128)(2,1)S(1)}, u32[]{:S(2)}, u32[]{:S(2)}) collective-permute-start(bf16[2048,128]{1,0:T(8,128)(2,1)} %get-tuple-element.14), channel_id=1, source_target_pairs={{0,1},{1,0},{2,3},{3,2},{4,5},{5,4},{6,7},{7,6},{8,9},{9,8},{10,11... | collective-permute-start | bytes 1572872 | tf_op jit(solution)/shard_map/ppermute | solution.py:363
  143.1 13.0 %copy-start = (bf16[4,768,128]{2,1,0:T(8,128)(2,1)}, bf16[4,768,128]{2,1,0:T(8,128)(2,1)S(1)}, u32[]{:S(2)}) copy-start(bf16[4,768,128]{2,1,0:T(8,128)(2,1)S(1)} %all-to-all-done.q_ref) | copy-start | bytes 2359300
  156.0 0.8 copy-start.5
  173.3 0.8 copy-start.4
  194.2 2.0 copy-start.1

commit v5 on v4

--- a/solution.py
+++ b/solution.py
@@ -293,7 +293,7 @@
     groups, rows, width = queries.shape
     heads, tokens, _ = values.shape
     per_head = groups // heads
-    block = math.gcd(rows, 256)
+    block = math.gcd(rows, 768)
     chunk = math.gcd(tokens, 1024)
     scale = 1.0 / math.sqrt(width)
     finish = part == parts - 1
@@ -323,35 +323,15 @@
     )(swap.reshape(1), queries, keys, values, *state)
 
 
-def stack_kernel(keys_ref, values_ref, out_ref):
-    width = out_ref.shape[2]
-    for head in range(out_ref.shape[0] // 2):
-        columns = slice(head * width, (head + 1) * width)
-        out_ref[2 * head] = keys_ref[:, columns]
-        out_ref[2 * head + 1] = values_ref[:, columns]
-
-
-def stack(keys, values, width):
-    rows, columns = keys.shape
-    pieces = 2 * columns // width
-    block = math.gcd(rows, 512)
-    spec = pl.BlockSpec((block, columns), lambda i: (i, 0))
-    return pl.pallas_call(
-        stack_kernel,
-        grid=(rows // block,),
-        in_specs=[spec, spec],
-        out_specs=pl.BlockSpec((pieces, block, width), lambda i: (0, i, 0)),
-        out_shape=jax.ShapeDtypeStruct((pieces, rows, width), keys.dtype),
-    )(keys, values)
-
-
 def by_pairs(keys, values, queries, positions, count):
     heads, rows, width = queries.shape
     me = lax.axis_index("ctx")
     odd = (me % 2).astype(jnp.int32)
-    mine = lax.all_to_all(
-        stack(keys, values, width), "ctx", split_axis=0, concat_axis=0, tiled=True
-    )
+    pieces = []
+    for head in range(heads):
+        pieces.append(keys[:, head * width : (head + 1) * width])
+        pieces.append(values[:, head * width : (head + 1) * width])
+    mine = lax.all_to_all(jnp.stack(pieces), "ctx", split_axis=0, concat_axis=0, tiled=True)
     rotated = rotate_rows(queries.astype(jnp.float32), positions.astype(jnp.float32)).astype(
         jnp.bfloat16
     )

time: 220 us -> 215 us (0.977)
  Pallas kernels: 73.1 us -> 63.9 us
  local copies, waits for them, and re-layouts: 4.67 us -> 7.1 us
  other arithmetic: 5.56 us -> 7.81 us
    pallas_call x1 -> x0, Pallas kernels: 6.77 us -> none  [stack(): pl.pallas_call(stack_kernel, grid=(rows // block,), in_specs=[spec, spec]...]
    pallas_call x2, Pallas kernels: 36.5 us -> 34 us  [attend(): pl.pallas_call(functools.partial(attend_kernel, chunk, scale, bool(state)...]
    another operation x0 -> x1, local copies, waits for them, and re-layouts: none -> 2.44 us  [by_pairs(): jnp.stack(pieces)]
    another operation x1 -> x2, other arithmetic: 0.39 us -> 2.65 us  [the longest x1 2.26 us: by_pairs(): jnp.stack(pieces)]
  transfers between devices with their start and end apart: 4 -> 4, of which waited for: 2 -> 2; matrix products, arithmetic and copies ran while one was open for 2% -> 2% of each run, Pallas kernels for 21% -> 19%
where the time goes in v5:
time: 215 us; the launch traced here: 214 us
  waiting for transfers between devices  102 us (47%)
  Pallas kernels  63.9 us (30%)
  blocking collectives  21 us (10%)
  starting transfers between devices  12.2 us (6%)
  other arithmetic  7.81 us (4%)
  local copies, waits for them, and re-layouts  7.1 us (3%)
    all_to_all x1, waiting for transfers between devices, by_pairs(): lax.all_to_all(jnp.stack(pieces), 'ctx', split_axis=0, concat_axis=0, til...  89.2 us
    pallas_call x2, Pallas kernels, attend(): pl.pallas_call(functools.partial(attend_kernel, chunk, scale, bool(state)...  34 us
    pallas_call x1, Pallas kernels, compress_rows(): pl.pallas_call(functools.partial(compress_kernel, inner), grid=(outer //...  29.9 us
    all_to_all x1, blocking collectives, by_pairs(): lax.all_to_all(jnp.concatenate([part, top, mid, last], axis=1), 'ctx', sp...  21 us
    ppermute x2, waiting for transfers between devices, by_pairs(): others = [lax.ppermute(send, 'ctx', pairs) for send in sends]  13 us
    all_to_all x1, starting transfers between devices, by_pairs(): lax.all_to_all(jnp.stack(pieces), 'ctx', split_axis=0, concat_axis=0, til...  6.48 us
  transfers between devices with their start and end apart: 4, of which 2 were waited for; matrix products, arithmetic and copies ran while one was open for 2% of the time, Pallas kernels for 19%

profile of v5, /device:TPU:0, one launch (start us, length us, event | category | flops | bytes accessed | tf_op | source)
XLA Modules:
  0.0 214.4 jit_solution(9811191890090881270)
XLA Ops:
  0.0 2.4 %slice_bitcast_fusion.2 = (bf16[1,4096,128]{2,1,0:T(8,128)(2,1)S(1)}, bf16[1,4096,128]{2,1,0:T(8,128)(2,1)S(1)}, bf16[1,4096,128]{2,1,0:T(8,128)(2,1)S(1)}, bf16[1,4096,128]{2,1,0:T(8,128)(2,1)S(1)}) fusion(bf16[4096,256]{1,0:T(8,128)(2,1)} %param.8, bf16[4096,256]{1,0:T(8,128)(2,1)} %param.7), kind=kLoop, calls=%fused_computation.4 | loop fusion | bytes 8388608 | tf_op jit(solution)/shard_map/stack | solution.py:334
  2.4 2.3 %pad_maximum_fusion = bf16[4,4096,128]{2,1,0:T(8,128)(2,1)} fusion(bf16[1,4096,128]{2,1,0:T(8,128)(2,1)S(1)} %get-tuple-element.24, bf16[1,4096,128]{2,1,0:T(8,128)(2,1)S(1)} %get-tuple-element.36, bf16[1,4096,128]{2,1,0:T(8,128)(2,1)S(1)} %get-tuple-element.23, bf16[1,4096,128]{2,1,0:T(8,128)(2,1)S(1)} %get-tuple-element.37), kind=kLoop, calls=%fused_computation | loop fusion | flops 6291456 | bytes 8388608 | tf_op jit(solution)/shard_map/stack | solution.py:334
  4.7 0.0 copy-start.3
  4.7 0.0 copy-start.2
  4.7 6.5 %all-to-all-start.1 = ((bf16[4,4096,128]{2,1,0:T(8,128)(2,1)}), bf16[4,4096,128]{2,1,0:T(8,128)(2,1)}, u32[]{:S(2)}, u32[]{:S(2)}) async-start(bf16[4,4096,128]{2,1,0:T(8,128)(2,1)} %pad_maximum_fusion), calls=%async_computation.1 | async-start | bytes 8388608 | tf_op jit(solution)/shard_map/all_to_all | solution.py:334
  11.2 0.0 copy-done.3
  11.2 0.0 copy-done.2
  11.2 0.1 convert_element_type.51
  11.3 0.2 multiply_cosine_fusion.2
  11.5 0.1 maximum_bitcast_fusion.2
  11.6 0.6 pad_maximum_fusion.4.fine_ref
  12.2 0.3 multiply_cosine_fusion.1
  12.5 0.1 maximum_bitcast_fusion
  12.6 0.7 pad_maximum_fusion.3.coarse_ref
  13.3 1.4 multiply_cosine_fusion
  14.7 0.4 subtract_convert_fusion
  15.1 0.2 pad_maximum_fusion.2
  15.4 89.2 %all-to-all-done.1 = bf16[4,4096,128]{2,1,0:T(8,128)(2,1)} async-done(((bf16[4,4096,128]{2,1,0:T(8,128)(2,1)}), bf16[4,4096,128]{2,1,0:T(8,128)(2,1)}, u32[]{:S(2)}, u32[]{:S(2)}) %all-to-all-start.1) | async-done | bytes 4194336 | tf_op jit(solution)/shard_map/all_to_all | solution.py:334
  104.6 1.0 broadcast_in_dim.8
  105.6 3.7 %all-to-all-start = ((bf16[4,768,128]{2,1,0:T(8,128)(2,1)}), bf16[4,768,128]{2,1,0:T(8,128)(2,1)S(1)}, u32[]{:S(2)}, u32[]{:S(2)}) async-start(bf16[4,768,128]{2,1,0:T(8,128)(2,1)} %bitcast.1), calls=%async_computation | async-start | bytes 1572864 | tf_op jit(solution)/shard_map/all_to_all | solution.py:338
  109.3 29.9 %shard_map.73 = (bf16[4096,128]{1,0:T(8,128)(2,1)}, bf16[2048,128]{1,0:T(8,128)(2,1)}, bf16[2048,128]{1,0:T(8,128)(2,1)}) custom-call(s32[1]{0:T(128)} %bitcast.odd_ref.swap_ref, bf16[16384,128]{1,0:T(8,128)(2,1)} %bitcast.6.x_ref, bf16[256,256]{1,0:T(8,128)(2,1)} %constant.35.clone.first_ref, bf16[128,256,256]{2,1,0:T(8,128)(2,1)} %constant.36.clone.middle_ref, ...), custom_call_target="tpu_custom_call" | custom-call | flops 17179869184 | bytes 33554432 | tf_op jit(solution)/shard_map/pallas_call | solution.py:212
  139.1 1.8 collective-permute-start.1
  140.9 0.2 collective-permute-start
  141.2 0.0 all-to-all-done.q_ref
  141.2 0.0 copy-start
  141.2 13.0 %collective-permute-done.1 = bf16[2048,128]{1,0:T(8,128)(2,1)S(1)} collective-permute-done((bf16[2048,128]{1,0:T(8,128)(2,1)}, bf16[2048,128]{1,0:T(8,128)(2,1)S(1)}, u32[]{:S(2)}, u32[]{:S(2)}) %collective-permute-start.1) | collective-permute-done | bytes 524320 | tf_op jit(solution)/shard_map/ppermute | solution.py:343
  154.2 0.0 copy-start.5
  154.2 0.0 copy-done
  154.2 0.8 copy-done.5
  155.0 11.5 %shard_map.74 = (f32[4,768,128]{2,1,0:T(8,128)}, f32[4,768,8]{2,1,0:T(8,128)}, f32[4,768,8]{2,1,0:T(8,128)}) custom-call(s32[1]{0:T(128)} %bitcast.odd_ref.swap_ref, bf16[4,768,128]{2,1,0:T(8,128)(2,1)} %copy-done, bf16[1,4096,128]{2,1,0:T(8,128)(2,1)} %bitcast.51, bf16[1,2048,128]{2,1,0:T(8,128)(2,1)} %bitcast.50), custom_call_target="tpu_custom_call" | custom-call | flops 6442450944 | bytes 3145728 | tf_op jit(solution)/shard_map/pallas_call | solution.py:305
  166.5 0.0 collective-permute-done
  166.5 0.0 copy-start.4
  166.5 0.8 copy-done.4
  167.3 22.5 %shard_map.75 = (bf16[4,768,128]{2,1,0:T(8,128)(2,1)}, f32[4,768,8]{2,1,0:T(8,128)}) custom-call(s32[1]{0:T(128)} %bitcast.odd_ref.swap_ref, bf16[4,768,128]{2,1,0:T(8,128)(2,1)} %copy-done, bf16[1,4096,128]{2,1,0:T(8,128)(2,1)} %bitcast.52, bf16[1,2048,128]{2,1,0:T(8,128)(2,1)} %bitcast.49, f32[4,768,128]{2,1,0:T(8,128)} %get-tuple-element.16.refs_0_, ...), custom_call_target="tpu_custom_call" | custom-call | flops 6442450944 | bytes 3145728 | tf_op jit(solution)/shard_map/pallas_call | solution.py:305
  189.8 0.0 copy-start.1
  189.8 2.0 slice_reduce_fusion
  191.8 0.0 copy-done.1
  191.8 0.1 pad_maximum_fusion.1
  191.9 21.0 %all_to_all.15 = bf16[4,786,128]{2,1,0:T(8,128)(2,1)S(1)} all-to-all(bf16[4,786,128]{2,1,0:T(8,128)(2,1)S(1)} %pad_maximum_fusion.1), channel_id=1, replica_groups=mesh['user'=4,'heads'=2,'ctx'=4] {'ctx'}, dimensions={0} | all-to-all | bytes 1609728 | tf_op jit(solution)/shard_map/all_to_all | solution.py:354
  213.0 0.1 slice.54
  213.1 0.1 convert.10
  213.2 1.2 fusion.2
  (12 shorter events, 0.1 us)
Async XLA Ops:
  4.7 6.5 %copy-start.3 = (s32[768]{0:T(1024)S(1)}, s32[768]{0:T(1024)}, u32[]{:S(2)}) copy-start(s32[768]{0:T(1024)} %param.10) | copy-start | bytes 9220
  4.7 6.5 %copy-start.2 = (bf16[2,768,128]{2,1,0:T(8,128)(2,1)S(1)}, bf16[2,768,128]{2,1,0:T(8,128)(2,1)}, u32[]{:S(2)}) copy-start(bf16[2,768,128]{2,1,0:T(8,128)(2,1)} %param.9) | copy-start | bytes 1179652
  4.7 99.9 %all-to-all-start.1 = ((bf16[4,4096,128]{2,1,0:T(8,128)(2,1)}), bf16[4,4096,128]{2,1,0:T(8,128)(2,1)}, u32[]{:S(2)}, u32[]{:S(2)}) async-start(bf16[4,4096,128]{2,1,0:T(8,128)(2,1)} %pad_maximum_fusion), calls=%async_computation.1 | async-start | bytes 8388608 | tf_op jit(solution)/shard_map/all_to_all | solution.py:334
  105.6 35.6 %all-to-all-start = ((bf16[4,768,128]{2,1,0:T(8,128)(2,1)}), bf16[4,768,128]{2,1,0:T(8,128)(2,1)S(1)}, u32[]{:S(2)}, u32[]{:S(2)}) async-start(bf16[4,768,128]{2,1,0:T(8,128)(2,1)} %bitcast.1), calls=%async_computation | async-start | bytes 1572864 | tf_op jit(solution)/shard_map/all_to_all | solution.py:338
  139.1 15.0 %collective-permute-start.1 = (bf16[2048,128]{1,0:T(8,128)(2,1)}, bf16[2048,128]{1,0:T(8,128)(2,1)S(1)}, u32[]{:S(2)}, u32[]{:S(2)}) collective-permute-start(bf16[2048,128]{1,0:T(8,128)(2,1)} %get-tuple-element.15), channel_id=1, source_target_pairs={{0,1},{1,0},{2,3},{3,2},{4,5},{5,4},{6,7},{7,6},{8,9},{9,8},{10,11... | collective-permute-start | bytes 1572872 | tf_op jit(solution)/shard_map/ppermute | solution.py:343
  140.9 25.6 %collective-permute-start = (bf16[2048,128]{1,0:T(8,128)(2,1)}, bf16[2048,128]{1,0:T(8,128)(2,1)S(1)}, u32[]{:S(2)}, u32[]{:S(2)}) collective-permute-start(bf16[2048,128]{1,0:T(8,128)(2,1)} %get-tuple-element.14), channel_id=1, source_target_pairs={{0,1},{1,0},{2,3},{3,2},{4,5},{5,4},{6,7},{7,6},{8,9},{9,8},{10,11... | collective-permute-start | bytes 1572872 | tf_op jit(solution)/shard_map/ppermute | solution.py:343
  141.2 13.0 %copy-start = (bf16[4,768,128]{2,1,0:T(8,128)(2,1)}, bf16[4,768,128]{2,1,0:T(8,128)(2,1)S(1)}, u32[]{:S(2)}) copy-start(bf16[4,768,128]{2,1,0:T(8,128)(2,1)S(1)} %all-to-all-done.q_ref) | copy-start | bytes 2359300
  154.2 0.8 copy-start.5
  166.5 0.8 copy-start.4
  189.8 2.0 copy-start.1
